TPU v7x, 32 devices: a whole 2x2x4 slice. The times are simulated.
32 devices in a mesh: groups: 1, orient: 8 (over z, core), cls: 4 (over y, x).
Axes of the slice: x: 2, y: 2, z: 4, core: 2. Of those that a mesh axis runs over, the one named last changes fastest.
Arguments:
- particles: bfloat16 [384, 33024], P(('groups', 'orient', 'cls')), may hold values from -300 to 300
- projections: bfloat16 [8, 8, 33024], P('cls', 'orient')
- ctf: bfloat16 [8, 16512], replicated, may hold values from -1 to 1
- defocus_group: int32 [384], P(('groups', 'orient', 'cls')), may hold values from 0 to 7
- offsets: int32 [384, 2], P(('groups', 'orient', 'cls')), may hold values from -8 to 8
- routes: int32 [384, 4], P(('groups', 'orient', 'cls')), may hold values from 0 to 7, all different within a row; in each aligned block of 12 rows (0 to 11, 12 to 23, ...) at most 6 rows name the same one
Outputs:
- log_evidence: float32 [384], P(('groups', 'orient', 'cls'))
- data_sum: bfloat16 [8, 8, 33024], P(('groups', 'cls'), 'orient')
Inputs may be any that keep to these rules, and one draw needn't show every extreme that they name: `routes`: the 4 blocks of a particle differ; among the particles of one device no block is listed more than 6 times, and some block is listed exactly 6 times.
All inputs are finite; a program needn't handle non-finite values.
Results may differ from a plain program's by a relative error of at most 0.01.
The roundings to bfloat16 on the way count: a program that leaves them out, or rounds other values in their place, can miss the bound.
Values may be sent and summed in bfloat16 or wider, within the bound.
No kernel may reach another device: no remote copies, remote signals or barrier semaphores. Data moves between devices by JAX's collectives and lax.ppermute only.
A program may use at most 64 MiB of HBM per device.

v0:
```python
import functools
import math

import jax
import jax.numpy as jnp
from jax import lax
from jax.experimental import pallas as pl
from jax.experimental.pallas import tpu as pltpu
from jax.sharding import Mesh
from jax.sharding import PartitionSpec as P


KX = 86
KY = 192
BOX = 256
LANES = 128
SHIFTS = 5

highest = lax.Precision.HIGHEST
f32 = jnp.float32
bf16 = jnp.bfloat16


def unit_circle(turns):
    quarter = BOX // 4
    quadrant = jnp.floor(turns * (1.0 / quarter) + 0.5)
    angle = (turns - quadrant * quarter) * (2.0 * math.pi / BOX)
    quadrant = quadrant - 4.0 * jnp.floor(quadrant * 0.25)
    square = angle * angle
    sine = angle * (
        1.0
        + square
        * (-1.0 / 6 + square * (1.0 / 120 + square * (-1.0 / 5040 + square * (1.0 / 362880))))
    )
    cosine = 1.0 + square * (
        -0.5 + square * (1.0 / 24 + square * (-1.0 / 720 + square * (1.0 / 40320)))
    )
    odd = (quadrant == 1.0) | (quadrant == 3.0)
    first = jnp.where(odd, sine, cosine)
    second = jnp.where(odd, cosine, sine)
    first = jnp.where((quadrant == 1.0) | (quadrant == 2.0), -first, first)
    second = jnp.where(quadrant >= 2.0, -second, second)
    return first, second


def other(place, step, size):
    if size & (size - 1) == 0:
        return place ^ step
    return lax.rem(place + step, size)


def source(place, step, size):
    if size & (size - 1) == 0:
        return place ^ step
    return lax.rem(place + size - step, size)


def exchange_order(step):
    return (step.bit_count() == 2, -step.bit_count(), step)


def routes_of(step, size):
    return [(i, int(other(i, step, size))) for i in range(size)]


def split_refs(pixel_count, width, refs, out):
    held = refs.shape[0]
    pieces = -(-pixel_count // width)
    for piece in range(pieces):
        low = piece * width
        size = min(width, pixel_count - low)
        for half in range(2):
            values = refs[:, half * pixel_count + low : half * pixel_count + low + size]
            for copy in range(piece, out.shape[0], pieces):
                out[copy, half * held : (half + 1) * held, 0:size] = values
                if size < width:
                    out[copy, half * held : (half + 1) * held, size:width] = jnp.zeros(
                        (held, width - size), bf16
                    )


def prepare_kernel(pixel_count, width, steps, *refs):
    distant, (place, split), rest = refs[:6], refs[6:8], refs[8:]
    outs, near, (ctf_rows, whole, table, arrived) = rest[: len(steps)], rest[len(steps) : -4], rest[-4:]
    copies = [
        pltpu.make_async_copy(far, here, arrived.at[i])
        for i, (far, here) in enumerate(zip(distant, near))
    ]
    for copy in copies:
        copy.start()
    copies[0].wait()
    split_refs(pixel_count, width, near[0], split)
    for copy in copies[1:]:
        copy.wait()
    align(pixel_count, width, steps, *near[1:], place, outs, ctf_rows, whole, table)


def align(
    pixel_count, width, steps, images, ctf, groups, offsets, routes, place, outs, ctf_rows, whole, table
):
    rows = images.shape[0]
    pieces = len(outs)
    route_count = routes.shape[0]
    table[...] = jnp.zeros(table.shape, f32)
    table[0:2, 0:rows] = offsets[...].astype(f32)
    table[2:3, 0:rows] = groups[...].astype(f32)
    table[3 : 3 + route_count, 0:rows] = routes[...].astype(f32)
    facts = table[...].T[0:rows]
    shift_across, shift_down, group = facts[:, 0:1], facts[:, 1:2], facts[:, 2:3]
    block = math.lcm(LANES, KY)
    per_block = block // LANES
    onehot = (
        group == lax.broadcasted_iota(jnp.int32, (rows, ctf.shape[0]), 1).astype(f32)
    ).astype(bf16)
    ctf_rows[...] = jnp.dot(onehot, ctf[...], preferred_element_type=f32)
    lane = lax.broadcasted_iota(jnp.int32, (rows, block), 1)
    across = jnp.zeros((rows, block), jnp.int32)
    for step in range(1, block // KY):
        across = across + (lane >= step * KY).astype(jnp.int32)
    down = lane - across * KY - KY // 2
    base_cos, base_sin = unit_circle(
        across.astype(f32) * shift_across + down.astype(f32) * shift_down
    )
    blocks = -(-pixel_count // block)
    start = lax.broadcasted_iota(jnp.int32, (rows, blocks), 1) * (block // KY)
    start_cos, start_sin = unit_circle(start.astype(f32) * shift_across)
    for piece in range(pieces):
        for part in range(width // LANES):
            low = piece * width + part * LANES
            here = slice(part * LANES, (part + 1) * LANES)
            if low >= pixel_count:
                whole[piece, :, here] = jnp.zeros((2 * rows, LANES), bf16)
                continue
            turn, step = divmod(low // LANES, per_block)
            bc = base_cos[:, step * LANES : (step + 1) * LANES]
            bs = base_sin[:, step * LANES : (step + 1) * LANES]
            rc = start_cos[:, turn : turn + 1]
            rs = start_sin[:, turn : turn + 1]
            cosine = bc * rc - bs * rs
            sine = bs * rc + bc * rs
            scale = ctf_rows[:, low : low + LANES]
            real = images[:, low : low + LANES].astype(f32)
            imag = images[:, pixel_count + low : pixel_count + low + LANES].astype(f32)
            first = (real * cosine + imag * sine) * scale
            second = (imag * cosine - real * sine) * scale
            whole[piece, :, here] = jnp.concatenate([first, second], axis=0).astype(bf16)
    lane = lax.broadcasted_iota(jnp.int32, (rows, LANES), 1)
    notes = jnp.where(lane == route_count, group, 0.0)
    for r in range(route_count):
        notes = jnp.where(lane == r, facts[:, 3 + r : 4 + r], notes)
    notes = jnp.concatenate([notes, notes], axis=0).astype(bf16)
    for step, out in zip(steps, outs):
        out[:, 0:width] = whole[other(place[0], step, pieces)]
        out[:, width : width + LANES] = notes


def lane_facts(total, owners, same_core, columns, core_here):
    lane = lax.broadcasted_iota(jnp.int32, (1, SHIFTS * total), 1)
    owner = lax.rem(lane, owners)
    core = source(core_here, owner // same_core, owners // same_core)
    direction = (lax.rem(owner, same_core) // columns) * (owners // same_core) + core
    shift, held = lane // total, lax.rem(lane, total) // owners
    spot = (shift * (total // owners) + held) * columns + lax.rem(owner, columns)
    return direction.astype(f32), spot.astype(f32)


def spot_table(spot, spots):
    row = lax.broadcasted_iota(jnp.int32, (spots, spot.shape[1]), 0).astype(f32)
    return jnp.where(row == spot, 1.0, 0.0).astype(bf16)


def score_kernel(rows, route_count, columns, steps, *refs_all):
    count = len(steps)
    parts = refs_all[:count]
    *blocks, ctf, phases, place, out, aligned, turned, power, dense, notes = refs_all[count:]
    same_core = blocks[0].shape[1]
    owners = len(blocks) * same_core
    width = phases.shape[1]
    held = blocks[0].shape[0] // 2
    total = held * len(blocks) * blocks[0].shape[1]
    for step, part in zip(steps, parts):
        aligned[source(place[0], step, count)] = part[...]
    for low in range(0, width, LANES):
        here = slice(low, low + LANES)
        real = jnp.concatenate(
            [block[k, :, here] for k in range(held) for block in blocks], axis=0
        )
        imag = jnp.concatenate(
            [block[held + k, :, here] for k in range(held) for block in blocks], axis=0
        )
        turned[0, 0:total, here] = real
        turned[1, 0:total, here] = imag
        real, imag = real.astype(f32), imag.astype(f32)
        power[:, here] = real * real + imag * imag
        for axis in range(2):
            cosine = phases[2 * axis : 2 * axis + 1, here]
            sine = phases[2 * axis + 1 : 2 * axis + 2, here]
            rc, rs, ic, is_ = real * cosine, real * sine, imag * cosine, imag * sine
            at = (1 + 2 * axis) * total
            turned[0, at : at + total, here] = (rc - is_).astype(bf16)
            turned[1, at : at + total, here] = (rs + ic).astype(bf16)
            at = at + total
            turned[0, at : at + total, here] = (rc + is_).astype(bf16)
            turned[1, at : at + total, here] = (ic - rs).astype(bf16)
    across = (((1,), (1,)), ((), ()))
    images = aligned[:, :, 0:width].reshape(2 * rows * count, width)
    real = lax.dot_general(images, turned[0], across, preferred_element_type=f32)
    imag = lax.dot_general(images, turned[1], across, preferred_element_type=f32)
    table = ctf[...].astype(f32)
    energy = lax.dot_general(
        table * table, power[...], across, precision=highest, preferred_element_type=f32
    )
    energy = jnp.concatenate([energy] * SHIFTS, axis=1) * 0.5
    for at in range(count):
        low = 2 * rows * at
        mine = slice(at * rows, (at + 1) * rows)
        dense[mine, :] = real[low : low + rows, :] + imag[low + rows : low + 2 * rows, :]
        notes[mine, :] = aligned[at, 0:rows, width : width + LANES].astype(f32)
    facts = notes[...]
    values = dense[...]
    for g in range(table.shape[0]):
        values = values - jnp.where(
            facts[:, route_count : route_count + 1] == float(g), energy[g : g + 1, :], 0.0
        )
    first = values.astype(bf16)
    rest = values - first.astype(f32)
    second = rest.astype(bf16)
    third = (rest - second.astype(f32)).astype(bf16)
    terms = [first.astype(f32), second.astype(f32), third.astype(f32)]
    direction, spot = lane_facts(total, owners, same_core, columns, place[1])
    spots = SHIFTS * held * columns
    choose = spot_table(spot, spots)
    height = out.shape[0]
    for r in range(route_count):
        listed = facts[:, r : r + 1] == direction
        chosen = jnp.zeros((rows * count, spots), f32)
        for term in terms:
            chosen = chosen + lax.dot_general(
                jnp.where(listed, term, 0.0).astype(bf16),
                choose,
                across,
                preferred_element_type=f32,
            )
        for block in range(rows * count // height):
            low = (block * route_count + r) * spots
            out[:, low : low + spots] = chosen[block * height : (block + 1) * height]


def sums_kernel(rows, route_count, columns, scores, aligned, phases, place, *outs_and_scratch):
    *outs, evidence, tall, wide = outs_and_scratch
    width = phases.shape[1]
    count = aligned.shape[0]
    cores = len(outs)
    same_core = outs[0].shape[1]
    owners = cores * same_core
    held = outs[0].shape[0] // 2
    total = held * owners
    height = scores.shape[0]
    blocks = count // (2 * height)
    listings = scores.shape[1] // blocks
    for block in range(blocks):
        tall[block * height : (block + 1) * height, :] = scores[
            :, block * listings : (block + 1) * listings
        ]
    for part in range(count // (2 * rows)):
        values = tall[part * rows : (part + 1) * rows, :]
        at = 2 * rows * part
        wide[at : at + rows, :] = values
        wide[at + rows : at + 2 * rows, :] = values
    values = wide[...]
    peak = jnp.max(values, axis=1, keepdims=True)
    mass = jnp.sum(jnp.exp(values - peak), axis=1, keepdims=True)
    log_evidence = peak + jnp.log(mass)
    evidence[...] = jnp.broadcast_to(log_evidence, evidence.shape)
    listed_weights = jnp.exp(values - log_evidence).astype(bf16)
    notes = aligned[:, width : width + LANES].astype(f32)
    direction, spot = lane_facts(total, owners, same_core, columns, place[1])
    spots = listings // route_count
    spread = spot_table(spot, spots)
    weights = jnp.zeros((count, SHIFTS * total), f32)
    for r in range(route_count):
        placed = jnp.dot(
            listed_weights[:, r * spots : (r + 1) * spots], spread, preferred_element_type=f32
        )
        weights = jnp.where(notes[:, r : r + 1] == direction, placed, weights)
    row = lax.broadcasted_iota(jnp.int32, (count, 1), 0)
    first_half = jnp.zeros((count, 1), jnp.bool_)
    for part in range(count // (2 * rows)):
        at = 2 * rows * part
        first_half = first_half | ((row >= at) & (row < at + rows))
    weights_real = jnp.where(first_half, weights, 0.0).T.astype(bf16)
    weights_imag = jnp.where(first_half, 0.0, weights).T.astype(bf16)
    chunk = 2 * LANES
    for low in range(0, width, chunk):
        high = min(low + chunk, width)
        images = aligned[:, low:high]
        real = jnp.dot(weights_real, images, preferred_element_type=f32)
        imag = jnp.dot(weights_imag, images, preferred_element_type=f32)
        u = [real[t * total : (t + 1) * total] for t in range(SHIFTS)]
        v = [imag[t * total : (t + 1) * total] for t in range(SHIFTS)]
        first, second = u[0], v[0]
        for axis in range(2):
            cosine = phases[2 * axis : 2 * axis + 1, low:high]
            sine = phases[2 * axis + 1 : 2 * axis + 2, low:high]
            one, two = 1 + 2 * axis, 2 + 2 * axis
            first = first + (u[one] + u[two]) * cosine + (v[one] - v[two]) * sine
            second = second + (v[one] + v[two]) * cosine - (u[one] - u[two]) * sine
        for k in range(held):
            for step, out in enumerate(outs):
                start = k * owners + step * same_core
                mine = slice(start, start + same_core)
                out[k, :, low:high] = first[mine].astype(out.dtype)
                out[held + k, :, low:high] = second[mine].astype(out.dtype)


def expectation(particles, projections, ctf, defocus_group, offsets, routes):
    pixel_count = KX * KY
    rows = particles.shape[0]
    route_count = routes.shape[1]
    held = projections.shape[0] * projections.shape[1]
    far, near, cores, columns = (
        lax.axis_size(name) for name in ("far", "near", "core", "cls")
    )
    group = ("near", "cls")
    same_core = ("far", "near", "cls")
    pieces = near * columns
    peers = far * pieces
    owners = peers * cores
    width = -(-pixel_count // (pieces * LANES)) * LANES
    padded = pieces * width
    place = lax.axis_index(group)
    total = held * owners
    params = pltpu.CompilerParams(vmem_limit_bytes=min(60 << 20, (8 << 20) + total * (88 << 10)))

    steps = [0] + sorted(range(1, pieces), key=exchange_order)
    where = jnp.stack([place, lax.axis_index("core")])
    scalars = pl.BlockSpec(memory_space=pltpu.SMEM)
    vectors = pl.BlockSpec(memory_space=pltpu.VMEM)
    distant = (
        projections.reshape(held, 2 * pixel_count),
        particles,
        ctf,
        defocus_group[None, :],
        offsets.T,
        routes.T,
    )
    piece = jax.ShapeDtypeStruct((2 * rows, width + LANES), bf16)
    refs, *parts = pl.pallas_call(
        functools.partial(prepare_kernel, pixel_count, width, steps),
        out_shape=[jax.ShapeDtypeStruct((peers, 2 * held, width), bf16)] + [piece] * pieces,
        in_specs=[pl.BlockSpec(memory_space=pltpu.HBM)] * len(distant) + [scalars],
        scratch_shapes=[pltpu.VMEM(array.shape, array.dtype) for array in distant]
        + [
            pltpu.VMEM((rows, pixel_count), f32),
            pltpu.VMEM((pieces, 2 * rows, width), bf16),
            pltpu.VMEM((-(-(3 + route_count) // 8) * 8, -(-rows // LANES) * LANES), f32),
            pltpu.SemaphoreType.DMA((len(distant),)),
        ],
        compiler_params=pltpu.CompilerParams(vmem_limit_bytes=60 << 20),
        name="prepare",
    )(*distant, where)
    refs = lax.all_to_all(refs, same_core, split_axis=0, concat_axis=0, tiled=True)
    blocks = [refs] + [lax.ppermute(refs, "core", routes_of(step, cores)) for step in range(1, cores)]
    blocks = [block.transpose(1, 0, 2) for block in blocks]
    parts = list(parts)
    for at in range(1, pieces):
        parts[at] = lax.ppermute(parts[at], group, routes_of(steps[at], pieces))

    column = place * width + jnp.arange(width, dtype=jnp.int32)
    across, down = column // KY, column % KY - KY // 2
    angles = jnp.stack([across, down]).astype(f32) * (2.0 * math.pi / BOX)
    phases = jnp.stack([jnp.cos(angles), jnp.sin(angles)], axis=1).reshape(4, width)
    ctf_here = lax.dynamic_slice_in_dim(
        jnp.pad(ctf, ((0, 0), (0, padded - pixel_count))), place * width, width, 1
    )

    count = pieces * rows
    listings = route_count * SHIFTS * held * columns
    folds = 4 if count % 32 == 0 else 1
    scores, aligned = pl.pallas_call(
        functools.partial(score_kernel, rows, route_count, columns, steps),
        out_shape=(
            jax.ShapeDtypeStruct((count // folds, folds * listings), f32),
            jax.ShapeDtypeStruct((pieces, 2 * rows, width + LANES), bf16),
        ),
        in_specs=[vectors] * (pieces + cores + 2) + [scalars],
        scratch_shapes=[
            pltpu.VMEM((2, SHIFTS * total, width), bf16),
            pltpu.VMEM((total, width), f32),
            pltpu.VMEM((count, SHIFTS * total), f32),
            pltpu.VMEM((count, LANES), f32),
        ],
        compiler_params=params,
        name="score",
    )(*parts, *blocks, ctf_here, phases, where)
    aligned = aligned.reshape(pieces * 2 * rows, width + LANES)

    span = 1
    while span < pieces:
        scores = scores + lax.ppermute(scores, group, [(i, i ^ span) for i in range(pieces)])
        span *= 2

    kinds = [f32] + [bf16] * (cores - 1)
    *sums, evidence = pl.pallas_call(
        functools.partial(sums_kernel, rows, route_count, columns),
        out_shape=(
            *(jax.ShapeDtypeStruct((2 * held, peers, width), kind) for kind in kinds),
            jax.ShapeDtypeStruct((2 * pieces * rows, LANES), f32),
        ),
        in_specs=[vectors] * 3 + [scalars],
        scratch_shapes=[pltpu.VMEM((count, listings), f32), pltpu.VMEM((2 * count, listings), f32)],
        compiler_params=params,
        name="sums",
    )(scores, aligned, phases, where)
    log_evidence = lax.dynamic_slice_in_dim(evidence, place * 2 * rows, rows, 0)[:, 0]

    merged = sums[0]
    for step in range(1, cores):
        merged = merged + lax.ppermute(sums[step], "core", routes_of(step, cores)).astype(f32)
    merged = merged.astype(bf16).transpose(1, 0, 2)
    merged = lax.all_to_all(merged, same_core, split_axis=0, concat_axis=0, tiled=True)
    data_sum = jnp.sum(merged.reshape(far, pieces, 2 * held, width).astype(f32), axis=0)
    data_sum = data_sum.astype(bf16).reshape(pieces, 2, held, width).transpose(2, 1, 0, 3)
    data_sum = data_sum.reshape(held, 2, padded)[:, :, :pixel_count]
    return (log_evidence, data_sum.reshape(projections.shape))


def solution(mesh):
    groups, orient, columns = (mesh.shape[name] for name in ("groups", "orient", "cls"))
    cores = 2 if orient % 2 == 0 else 1
    near = 2 if orient % (2 * cores) == 0 else 1
    axes = ("groups", "far", "near", "core", "cls")
    along = ("far", "near", "core")
    inner = Mesh(
        mesh.devices.reshape(groups, orient // (near * cores), near, cores, columns), axes
    )
    placed = (
        P(axes, None),
        P("cls", along, None),
        P(),
        P(axes),
        P(axes, None),
        P(axes, None),
    )
    return jax.shard_map(
        expectation,
        mesh=inner,
        in_specs=placed,
        out_specs=(P(axes), P(("groups", "cls"), along, None)),
        check_vma=False,
    )
```

profile of v0, /device:TPU:0, one launch (start us, length us, event | category | flops | bytes accessed | tf_op | source)
XLA Modules:
  0.0 70.4 jit_solution(3163179496899333730)
XLA Ops:
  0.6 0.6 pad_add_fusion.refs_6_.refs_all_12_.place
  1.3 4.0 %prepare.1 = (bf16[16,4,2176]{2,1,0:T(4,128)(2,1)}, bf16[24,2304]{1,0:T(8,128)(2,1)}, bf16[24,2304]{1,0:T(8,128)(2,1)}, bf16[24,2304]{1,0:T(8,128)(2,1)}, bf16[2...) custom-call(bf16[2,33024]{1,0:T(2,128)(2,1)} %bitcast.30, ...), custom_call_target="tpu_custom_call" | custom-call | tf_op jit(solution)/shard_map/prepare/pallas_call | solution.py:348
  5.3 8.5 %all-to-all-start = ((bf16[16,4,2176]{2,1,0:T(4,128)(2,1)}), bf16[16,4,2176]{2,1,0:T(4,128)(2,1)S(1)}, u32[]{:S(2)}, u32[]{:S(2)}) async-start(bf16[16,4,2176]{2,1,0:T(4,128)(2,1)} %get-tuple-element.24), calls=%async_computation | async-start | bytes 557056 | tf_op jit(solution)/shard_map/all_to_all | solution.py:362
  13.7 3.7 %collective-permute-start = (bf16[24,2304]{1,0:T(8,128)(2,1)}, bf16[24,2304]{1,0:T(8,128)(2,1)S(1)}, u32[]{:S(2)}, u32[]{:S(2)}) collective-permute-start(bf16[24,2304]{1,0:T(8,128)(2,1)} %get-tuple-element.17), channel_id=1, source_target_pairs={{0,11},{1,10},{2,9},{3,8},{8,3},{9,2},{10,1},{11,0},{4,15},{5,14},... | collective-permute-start | bytes 331784 | tf_op jit(solution)/shard_map/ppermute | solution.py:367
  17.5 0.6 collective-permute-start.1
  18.0 0.6 collective-permute-start.2
  18.6 0.2 collective-permute-start.3
  18.8 2.8 %collective-permute-start.4 = (bf16[24,2304]{1,0:T(8,128)(2,1)}, bf16[24,2304]{1,0:T(8,128)(2,1)S(1)}, u32[]{:S(2)}, u32[]{:S(2)}) collective-permute-start(bf16[24,2304]{1,0:T(8,128)(2,1)} %get-tuple-element.21), channel_id=1, source_target_pairs={{0,3},{1,2},{2,1},{3,0},{8,11},{9,10},{10,9},{11,8},{4,7},{5,6},{6... | collective-permute-start | bytes 331784 | tf_op jit(solution)/shard_map/ppermute | solution.py:367
  21.6 0.1 fusion.3
  21.7 0.5 fusion.7
  22.2 2.5 %all-to-all-done = bf16[16,4,2176]{2,1,0:T(4,128)(2,1)S(1)} async-done(((bf16[16,4,2176]{2,1,0:T(4,128)(2,1)}), bf16[16,4,2176]{2,1,0:T(4,128)(2,1)S(1)}, u32[]{:S(2)}, u32[]{:S(2)}) %all-to-all-start) | async-done | bytes 278560 | tf_op jit(solution)/shard_map/all_to_all | solution.py:362
  24.7 1.0 %collective-permute-done.refs_all_1_ = bf16[24,2304]{1,0:T(8,128)(2,1)S(1)} collective-permute-done((bf16[24,2304]{1,0:T(8,128)(2,1)}, bf16[24,2304]{1,0:T(8,128)(2,1)S(1)}, u32[]{:S(2)}, u32[]{:S(2)}) %collective-permute-start) | collective-permute-done | bytes 110624 | tf_op jit(solution)/shard_map/ppermute | solution.py:367
  25.7 0.7 collective-permute-start.5
  26.4 2.8 %collective-permute-start.6 = (bf16[24,2304]{1,0:T(8,128)(2,1)S(1)}, bf16[24,2304]{1,0:T(8,128)(2,1)S(1)}, u32[]{:S(2)}, u32[]{:S(2)}) collective-permute-start(bf16[24,2304]{1,0:T(8,128)(2,1)S(1)} %copy-done.3), channel_id=1, source_target_pairs={{0,10},{1,11},{2,8},{3,9},{8,2},{9,3},{10,0},{11,1},{4,14},{5,15},... | collective-permute-start | bytes 331784 | tf_op jit(solution)/shard_map/ppermute | solution.py:367
  29.2 0.5 collective-permute-done.4.refs_all_5_
  29.7 1.6 %collective-permute-done.5.refs_all_6_ = bf16[24,2304]{1,0:T(8,128)(2,1)S(1)} collective-permute-done((bf16[24,2304]{1,0:T(8,128)(2,1)S(1)}, bf16[24,2304]{1,0:T(8,128)(2,1)S(1)}, u32[]{:S(2)}, u32[]{:S(2)}) %collective-permute-start.5) | collective-permute-done | bytes 110624 | tf_op jit(solution)/shard_map/ppermute | solution.py:367
  31.3 0.7 %collective-permute-done.6.refs_all_7_ = bf16[24,2304]{1,0:T(8,128)(2,1)S(1)} collective-permute-done((bf16[24,2304]{1,0:T(8,128)(2,1)S(1)}, bf16[24,2304]{1,0:T(8,128)(2,1)S(1)}, u32[]{:S(2)}, u32[]{:S(2)}) %collective-permute-start.6) | collective-permute-done | bytes 110624 | tf_op jit(solution)/shard_map/ppermute | solution.py:367
  32.1 3.5 %score.1 = (f32[24,640]{1,0:T(8,128)S(1)}, bf16[8,24,2304]{2,1,0:T(8,128)(2,1)S(1)}) custom-call(bf16[24,2304]{1,0:T(8,128)(2,1)S(1)} %copy-done, bf16[24,2304]{1,0:T(8,128)(2,1)S(1)} %collective-permute-done.refs_all_1_, bf16[24,2304]{1,0:T(8,128)(2,1)S(1)} %collective-permute-done.1.refs_all_2_, bf16[24,2304]{1,0:T(8,128)(2,1)S(1)} %collective-permute-done.2.refs_all_3_, ...), custom_call_target="tpu_custom_call" | custom-call | tf_op jit(solution)/shard_map/score/pallas_call | solution.py:380
  35.6 1.5 %collective-permute-start.8 = (f32[24,640]{1,0:T(8,128)S(1)}, f32[24,640]{1,0:T(8,128)S(1)}, u32[]{:S(2)}, u32[]{:S(2)}) collective-permute-start(f32[24,640]{1,0:T(8,128)S(1)} %get-tuple-element.25), channel_id=1, source_target_pairs={{0,1},{1,0},{2,3},{3,2},{8,9},{9,8},{10,11},{11,10},{4,5},{5,4},{6... | collective-permute-start | bytes 184328 | tf_op jit(solution)/shard_map/ppermute | solution.py:400
  37.1 2.8 %collective-permute-done.8 = f32[24,640]{1,0:T(8,128)S(1)} collective-permute-done((f32[24,640]{1,0:T(8,128)S(1)}, f32[24,640]{1,0:T(8,128)S(1)}, u32[]{:S(2)}, u32[]{:S(2)}) %collective-permute-start.8) | collective-permute-done | bytes 61472 | tf_op jit(solution)/shard_map/ppermute | solution.py:400
  39.9 1.1 %collective-permute-start.9 = (f32[24,640]{1,0:T(8,128)S(1)}, f32[24,640]{1,0:T(8,128)S(1)}, u32[]{:S(2)}, u32[]{:S(2)}) collective-permute-start(f32[24,640]{1,0:T(8,128)S(1)} %add.104), channel_id=1, source_target_pairs={{0,2},{1,3},{2,0},{3,1},{8,10},{9,11},{10,8},{11,9},{4,6},{5,7},{6... | collective-permute-start | bytes 184328 | tf_op jit(solution)/shard_map/ppermute | solution.py:400
  41.0 3.2 %collective-permute-done.9 = f32[24,640]{1,0:T(8,128)S(1)} collective-permute-done((f32[24,640]{1,0:T(8,128)S(1)}, f32[24,640]{1,0:T(8,128)S(1)}, u32[]{:S(2)}, u32[]{:S(2)}) %collective-permute-start.9) | collective-permute-done | bytes 61472 | tf_op jit(solution)/shard_map/ppermute | solution.py:400
  44.2 1.4 %collective-permute-start.10 = (f32[24,640]{1,0:T(8,128)S(1)}, f32[24,640]{1,0:T(8,128)S(1)}, u32[]{:S(2)}, u32[]{:S(2)}) collective-permute-start(f32[24,640]{1,0:T(8,128)S(1)} %add.105), channel_id=1, source_target_pairs={{0,8},{1,9},{2,10},{3,11},{8,0},{9,1},{10,2},{11,3},{4,12},{5,13},... | collective-permute-start | bytes 184328 | tf_op jit(solution)/shard_map/ppermute | solution.py:400
  45.5 2.9 %collective-permute-done.10 = f32[24,640]{1,0:T(8,128)S(1)} collective-permute-done((f32[24,640]{1,0:T(8,128)S(1)}, f32[24,640]{1,0:T(8,128)S(1)}, u32[]{:S(2)}, u32[]{:S(2)}) %collective-permute-start.10) | collective-permute-done | bytes 61472 | tf_op jit(solution)/shard_map/ppermute | solution.py:400
  48.5 2.2 %sums.1 = (f32[4,16,2176]{2,1,0:T(8,128)S(1)}, bf16[4,16,2176]{2,1,0:T(8,128)(2,1)S(1)}, f32[192,128]{1,0:T(8,128)S(1)}) custom-call(f32[24,640]{1,0:T(8,128)S(1)} %add.106.scores, bf16[192,2304]{1,0:T(8,128)(2,1)S(1)} %bitcast.26, f32[4,2176]{1,0:T(4,128)S(1)} %reshape.113.refs_all_11_.phases, s32[2]{0:T(128)S(1)} %copy-done.1), custom_call_target="tpu_custom_call" | custom-call | tf_op jit(solution)/shard_map/sums/pallas_call | solution.py:404
  50.7 1.5 %collective-permute-done.11 = bf16[4,16,2176]{2,1,0:T(8,128)(2,1)S(1)} collective-permute-done((bf16[4,16,2176]{2,1,0:T(8,128)(2,1)S(1)}, bf16[4,16,2176]{2,1,0:T(8,128)(2,1)S(1)}, u32[]{:S(2)}, u32[]{:S(2)}) %collective-permute-start.11) | collective-permute-done | bytes 278560 | tf_op jit(solution)/shard_map/ppermute | solution.py:419
  52.3 0.8 %copy.17 = bf16[16,4,2176]{2,1,0:T(4,128)(2,1)} copy(bf16[16,4,2176]{2,0,1:T(8,128)(2,1)S(1)} %fusion) | data formatting | bytes 557056 | tf_op jit(solution)/shard_map/transpose | solution.py:420
  53.1 5.6 %all-to-all-start.1 = ((bf16[16,4,2176]{2,1,0:T(4,128)(2,1)}), bf16[16,4,2176]{2,1,0:T(4,128)(2,1)S(1)}, u32[]{:S(2)}, u32[]{:S(2)}) async-start(bf16[16,4,2176]{2,1,0:T(4,128)(2,1)} %copy.17), calls=%async_computation.1 | async-start | bytes 557056 | tf_op jit(solution)/shard_map/all_to_all | solution.py:421
  58.7 0.6 dynamic-slice_reduce_fusion
  59.3 10.0 %all-to-all-done.1 = bf16[16,4,2176]{2,1,0:T(4,128)(2,1)S(1)} async-done(((bf16[16,4,2176]{2,1,0:T(4,128)(2,1)}), bf16[16,4,2176]{2,1,0:T(4,128)(2,1)S(1)}, u32[]{:S(2)}, u32[]{:S(2)}) %all-to-all-start.1) | async-done | bytes 278560 | tf_op jit(solution)/shard_map/all_to_all | solution.py:421
  69.4 0.2 reduce_sum.12
  69.7 0.7 %slice.8 = bf16[2,2,16512]{2,0,1:T(2,128)(2,1)} slice(bf16[2,2,17408]{2,0,1:T(2,128)(2,1)S(1)} %reshape.117), slice={[0:2], [0:2], [0:16512]} | slice | bytes 264192 | tf_op jit(solution)/shard_map/slice | solution.py:424
  (26 shorter events, 0.4 us)
Async XLA Ops:
  0.6 20.9 %copy-start.2 = (bf16[8,16512]{1,0:T(8,128)(2,1)S(1)}, bf16[8,16512]{1,0:T(8,128)(2,1)}, u32[]{:S(2)}) copy-start(bf16[8,16512]{1,0:T(8,128)(2,1)} %refs_2_.1) | copy-start | bytes 792580
  5.2 20.5 %copy-start.4 = (bf16[24,2304]{1,0:T(8,128)(2,1)S(1)}, bf16[24,2304]{1,0:T(8,128)(2,1)}, u32[]{:S(2)}) copy-start(bf16[24,2304]{1,0:T(8,128)(2,1)} %get-tuple-element.22) | copy-start | bytes 331780
  5.2 21.2 %copy-start.3 = (bf16[24,2304]{1,0:T(8,128)(2,1)S(1)}, bf16[24,2304]{1,0:T(8,128)(2,1)}, u32[]{:S(2)}) copy-start(bf16[24,2304]{1,0:T(8,128)(2,1)} %get-tuple-element.23) | copy-start | bytes 331780
  5.2 26.8 %copy-start = (bf16[24,2304]{1,0:T(8,128)(2,1)S(1)}, bf16[24,2304]{1,0:T(8,128)(2,1)}, u32[]{:S(2)}) copy-start(bf16[24,2304]{1,0:T(8,128)(2,1)} %get-tuple-element.16.refs_all_0_) | copy-start | bytes 331780
  5.2 26.8 %copy-start.1 = (s32[2]{0:T(128)S(1)}, s32[2]{0:T(128)}, u32[]{:S(2)}) copy-start(s32[2]{0:T(128)} %pad_add_fusion.refs_6_.refs_all_12_.place) | copy-start | bytes 28
  5.3 19.4 %all-to-all-start = ((bf16[16,4,2176]{2,1,0:T(4,128)(2,1)}), bf16[16,4,2176]{2,1,0:T(4,128)(2,1)S(1)}, u32[]{:S(2)}, u32[]{:S(2)}) async-start(bf16[16,4,2176]{2,1,0:T(4,128)(2,1)} %get-tuple-element.24), calls=%async_computation | async-start | bytes 557056 | tf_op jit(solution)/shard_map/all_to_all | solution.py:362
  13.7 11.9 %collective-permute-start = (bf16[24,2304]{1,0:T(8,128)(2,1)}, bf16[24,2304]{1,0:T(8,128)(2,1)S(1)}, u32[]{:S(2)}, u32[]{:S(2)}) collective-permute-start(bf16[24,2304]{1,0:T(8,128)(2,1)} %get-tuple-element.17), channel_id=1, source_target_pairs={{0,11},{1,10},{2,9},{3,8},{8,3},{9,2},{10,1},{11,0},{4,15},{5,14},... | collective-permute-start | bytes 331784 | tf_op jit(solution)/shard_map/ppermute | solution.py:367
  17.5 8.9 %collective-permute-start.1 = (bf16[24,2304]{1,0:T(8,128)(2,1)}, bf16[24,2304]{1,0:T(8,128)(2,1)S(1)}, u32[]{:S(2)}, u32[]{:S(2)}) collective-permute-start(bf16[24,2304]{1,0:T(8,128)(2,1)} %get-tuple-element.18), channel_id=1, source_target_pairs={{0,1},{1,0},{2,3},{3,2},{8,9},{9,8},{10,11},{11,10},{4,5},{5,4},{6... | collective-permute-start | bytes 331784 | tf_op jit(solution)/shard_map/ppermute | solution.py:367
  18.0 11.1 %collective-permute-start.2 = (bf16[24,2304]{1,0:T(8,128)(2,1)}, bf16[24,2304]{1,0:T(8,128)(2,1)S(1)}, u32[]{:S(2)}, u32[]{:S(2)}) collective-permute-start(bf16[24,2304]{1,0:T(8,128)(2,1)} %get-tuple-element.19), channel_id=1, source_target_pairs={{0,2},{1,3},{2,0},{3,1},{8,10},{9,11},{10,8},{11,9},{4,6},{5,7},{6... | collective-permute-start | bytes 331784 | tf_op jit(solution)/shard_map/ppermute | solution.py:367
  18.6 10.6 %collective-permute-start.3 = (bf16[24,2304]{1,0:T(8,128)(2,1)}, bf16[24,2304]{1,0:T(8,128)(2,1)S(1)}, u32[]{:S(2)}, u32[]{:S(2)}) collective-permute-start(bf16[24,2304]{1,0:T(8,128)(2,1)} %get-tuple-element.20), channel_id=1, source_target_pairs={{0,8},{1,9},{2,10},{3,11},{8,0},{9,1},{10,2},{11,3},{4,12},{5,13},... | collective-permute-start | bytes 331784 | tf_op jit(solution)/shard_map/ppermute | solution.py:367
  18.8 10.9 %collective-permute-start.4 = (bf16[24,2304]{1,0:T(8,128)(2,1)}, bf16[24,2304]{1,0:T(8,128)(2,1)S(1)}, u32[]{:S(2)}, u32[]{:S(2)}) collective-permute-start(bf16[24,2304]{1,0:T(8,128)(2,1)} %get-tuple-element.21), channel_id=1, source_target_pairs={{0,3},{1,2},{2,1},{3,0},{8,11},{9,10},{10,9},{11,8},{4,7},{5,6},{6... | collective-permute-start | bytes 331784 | tf_op jit(solution)/shard_map/ppermute | solution.py:367
  25.7 5.6 %collective-permute-start.5 = (bf16[24,2304]{1,0:T(8,128)(2,1)S(1)}, bf16[24,2304]{1,0:T(8,128)(2,1)S(1)}, u32[]{:S(2)}, u32[]{:S(2)}) collective-permute-start(bf16[24,2304]{1,0:T(8,128)(2,1)S(1)} %copy-done.4), channel_id=1, source_target_pairs={{0,9},{1,8},{2,11},{3,10},{8,1},{9,0},{10,3},{11,2},{4,13},{5,12},... | collective-permute-start | bytes 331784 | tf_op jit(solution)/shard_map/ppermute | solution.py:367
  26.4 5.6 %collective-permute-start.6 = (bf16[24,2304]{1,0:T(8,128)(2,1)S(1)}, bf16[24,2304]{1,0:T(8,128)(2,1)S(1)}, u32[]{:S(2)}, u32[]{:S(2)}) collective-permute-start(bf16[24,2304]{1,0:T(8,128)(2,1)S(1)} %copy-done.3), channel_id=1, source_target_pairs={{0,10},{1,11},{2,8},{3,9},{8,2},{9,3},{10,0},{11,1},{4,14},{5,15},... | collective-permute-start | bytes 331784 | tf_op jit(solution)/shard_map/ppermute | solution.py:367
  29.2 2.9 %collective-permute-start.7 = (bf16[16,4,2176]{2,0,1:T(8,128)(2,1)S(1)}, bf16[16,4,2176]{2,0,1:T(8,128)(2,1)S(1)}, u32[]{:S(2)}, u32[]{:S(2)}) collective-permute-start(bf16[16,4,2176]{2,0,1:T(8,128)(2,1)S(1)} %copy.22), channel_id=1, source_target_pairs={{0,4},{4,0},{1,5},{5,1},{2,6},{6,2},{3,7},{7,3},{8,12},{12,8},{9,1... | collective-permute-start | bytes 835592 | tf_op jit(solution)/shard_map/ppermute | solution.py:363
  35.6 4.3 %collective-permute-start.8 = (f32[24,640]{1,0:T(8,128)S(1)}, f32[24,640]{1,0:T(8,128)S(1)}, u32[]{:S(2)}, u32[]{:S(2)}) collective-permute-start(f32[24,640]{1,0:T(8,128)S(1)} %get-tuple-element.25), channel_id=1, source_target_pairs={{0,1},{1,0},{2,3},{3,2},{8,9},{9,8},{10,11},{11,10},{4,5},{5,4},{6... | collective-permute-start | bytes 184328 | tf_op jit(solution)/shard_map/ppermute | solution.py:400
  39.9 4.3 %collective-permute-start.9 = (f32[24,640]{1,0:T(8,128)S(1)}, f32[24,640]{1,0:T(8,128)S(1)}, u32[]{:S(2)}, u32[]{:S(2)}) collective-permute-start(f32[24,640]{1,0:T(8,128)S(1)} %add.104), channel_id=1, source_target_pairs={{0,2},{1,3},{2,0},{3,1},{8,10},{9,11},{10,8},{11,9},{4,6},{5,7},{6... | collective-permute-start | bytes 184328 | tf_op jit(solution)/shard_map/ppermute | solution.py:400
  44.2 4.3 %collective-permute-start.10 = (f32[24,640]{1,0:T(8,128)S(1)}, f32[24,640]{1,0:T(8,128)S(1)}, u32[]{:S(2)}, u32[]{:S(2)}) collective-permute-start(f32[24,640]{1,0:T(8,128)S(1)} %add.105), channel_id=1, source_target_pairs={{0,8},{1,9},{2,10},{3,11},{8,0},{9,1},{10,2},{11,3},{4,12},{5,13},... | collective-permute-start | bytes 184328 | tf_op jit(solution)/shard_map/ppermute | solution.py:400
  50.6 1.6 %collective-permute-start.11 = (bf16[4,16,2176]{2,1,0:T(8,128)(2,1)S(1)}, bf16[4,16,2176]{2,1,0:T(8,128)(2,1)S(1)}, u32[]{:S(2)}, u32[]{:S(2)}) collective-permute-start(bf16[4,16,2176]{2,1,0:T(8,128)(2,1)S(1)} %get-tuple-element.29), channel_id=1, source_target_pairs={{0,4},{4,0},{1,5},{5,1},{2,6},{6,2},{3,7},{7,3},{8,12},{12,8},{9,1... | collective-permute-start | bytes 835592 | tf_op jit(solution)/shard_map/ppermute | solution.py:419
  53.1 16.2 %all-to-all-start.1 = ((bf16[16,4,2176]{2,1,0:T(4,128)(2,1)}), bf16[16,4,2176]{2,1,0:T(4,128)(2,1)S(1)}, u32[]{:S(2)}, u32[]{:S(2)}) async-start(bf16[16,4,2176]{2,1,0:T(4,128)(2,1)} %copy.17), calls=%async_computation.1 | async-start | bytes 557056 | tf_op jit(solution)/shard_map/all_to_all | solution.py:421
where the time goes:
time: 70.8 us; the launch traced here: 70.4 us
  starting transfers between devices  29.4 us (42%)
  waiting for transfers between devices  26.7 us (38%)
  Pallas kernels  9.62 us (14%)
  local copies, waits for them, and re-layouts  2.36 us (3%)
  other arithmetic  1.55 us (2%)
  between operations  0.82 us (1%)
    ppermute x7, starting transfers between devices, expectation(): parts[at] = lax.ppermute(parts[at], group, routes_of(steps[at], pieces))  11.2 us
    all_to_all x1, waiting for transfers between devices, expectation(): lax.all_to_all(merged, same_core, split_axis=0, concat_axis=0, tiled=True)  10 us
    ppermute x3, waiting for transfers between devices, expectation(): lax.ppermute(scores, group, [(i, i ^ span) for i in range(pieces)])  8.83 us
    all_to_all x1, starting transfers between devices, expectation(): lax.all_to_all(refs, same_core, split_axis=0, concat_axis=0, tiled=True)  8.48 us
    all_to_all x1, starting transfers between devices, expectation(): lax.all_to_all(merged, same_core, split_axis=0, concat_axis=0, tiled=True)  5.56 us
    ppermute x3, starting transfers between devices, expectation(): lax.ppermute(scores, group, [(i, i ^ span) for i in range(pieces)])  4.02 us
    pallas_call x1, Pallas kernels, expectation(): pl.pallas_call(functools.partial(prepare_kernel, pixel_count, width, step...  3.95 us
    ppermute x7, waiting for transfers between devices, expectation(): parts[at] = lax.ppermute(parts[at], group, routes_of(steps[at], pieces))  3.77 us
  transfers between devices with their start and end apart: 14, of which 10 were waited for; matrix products, arithmetic and copies ran while one was open for 2% of the time, Pallas kernels for 0%

commit v1 on v0

--- a/solution.py
+++ b/solution.py
@@ -172,7 +172,9 @@
 def score_kernel(rows, route_count, columns, steps, *refs_all):
     count = len(steps)
     parts = refs_all[:count]
-    *blocks, ctf, phases, place, out, aligned, turned, power, dense, notes = refs_all[count:]
+    *blocks, ctf, phases, place, out, aligned, turned, power, dense, notes, packed = (
+        refs_all[count:]
+    )
     same_core = blocks[0].shape[1]
     owners = len(blocks) * same_core
     width = phases.shape[1]
@@ -229,21 +231,28 @@
     terms = [first.astype(f32), second.astype(f32), third.astype(f32)]
     direction, spot = lane_facts(total, owners, same_core, columns, place[1])
     spots = SHIFTS * held * columns
-    choose = spot_table(spot, spots)
-    height = out.shape[0]
+    particles = rows * count
+    stacked = []
     for r in range(route_count):
         listed = facts[:, r : r + 1] == direction
-        chosen = jnp.zeros((rows * count, spots), f32)
-        for term in terms:
-            chosen = chosen + lax.dot_general(
-                jnp.where(listed, term, 0.0).astype(bf16),
-                choose,
-                across,
-                preferred_element_type=f32,
-            )
-        for block in range(rows * count // height):
-            low = (block * route_count + r) * spots
-            out[:, low : low + spots] = chosen[block * height : (block + 1) * height]
+        stacked += [jnp.where(listed, term, 0.0).astype(bf16) for term in terms]
+    chosen = lax.dot_general(
+        jnp.concatenate(stacked, axis=0),
+        spot_table(spot, spots),
+        across,
+        preferred_element_type=f32,
+    )
+    height = out.shape[1]
+    for r in range(route_count):
+        low = r * len(terms) * particles
+        mine = chosen[low : low + particles]
+        for term in range(1, len(terms)):
+            mine = mine + chosen[low + term * particles : low + (term + 1) * particles]
+        for block in range(particles // height):
+            at = (block * route_count + r) * spots
+            packed[:, at : at + spots] = mine[block * height : (block + 1) * height]
+    for copy in range(out.shape[0]):
+        out[copy] = packed[...]
 
 
 def sums_kernel(rows, route_count, columns, scores, aligned, phases, place, *outs_and_scratch):
@@ -255,11 +264,14 @@
     owners = cores * same_core
     held = outs[0].shape[0] // 2
     total = held * owners
-    height = scores.shape[0]
+    height = scores.shape[1]
     blocks = count // (2 * height)
-    listings = scores.shape[1] // blocks
+    listings = scores.shape[2] // blocks
+    summed = scores[0]
+    for part in range(1, scores.shape[0]):
+        summed = summed + scores[part]
     for block in range(blocks):
-        tall[block * height : (block + 1) * height, :] = scores[
+        tall[block * height : (block + 1) * height, :] = summed[
             :, block * listings : (block + 1) * listings
         ]
     for part in range(count // (2 * rows)):
@@ -380,7 +392,7 @@
     scores, aligned = pl.pallas_call(
         functools.partial(score_kernel, rows, route_count, columns, steps),
         out_shape=(
-            jax.ShapeDtypeStruct((count // folds, folds * listings), f32),
+            jax.ShapeDtypeStruct((pieces, count // folds, folds * listings), f32),
             jax.ShapeDtypeStruct((pieces, 2 * rows, width + LANES), bf16),
         ),
         in_specs=[vectors] * (pieces + cores + 2) + [scalars],
@@ -389,16 +401,14 @@
             pltpu.VMEM((total, width), f32),
             pltpu.VMEM((count, SHIFTS * total), f32),
             pltpu.VMEM((count, LANES), f32),
+            pltpu.VMEM((count // folds, folds * listings), f32),
         ],
         compiler_params=params,
         name="score",
     )(*parts, *blocks, ctf_here, phases, where)
     aligned = aligned.reshape(pieces * 2 * rows, width + LANES)
 
-    span = 1
-    while span < pieces:
-        scores = scores + lax.ppermute(scores, group, [(i, i ^ span) for i in range(pieces)])
-        span *= 2
+    scores = lax.all_to_all(scores, group, split_axis=0, concat_axis=0, tiled=True)
 
     kinds = [f32] + [bf16] * (cores - 1)
     *sums, evidence = pl.pallas_call(

time: 70.8 us -> 67.9 us (0.959)
  blocking collectives: 0 us -> 11.7 us
  waiting for transfers between devices: 26.7 us -> 18 us
  starting transfers between devices: 29.4 us -> 23.5 us
    all_to_all x0 -> x1, blocking collectives: none -> 11.7 us  [expectation(): lax.all_to_all(scores, group, split_axis=0, concat_axis=0, tiled=True)]
    ppermute x3 -> x0, waiting for transfers between devices: 8.83 us -> none  [expectation(): lax.ppermute(scores, group, [(i, i ^ span) for i in range(pieces)])]
    ppermute x3 -> x0, starting transfers between devices: 4.02 us -> none  [expectation(): lax.ppermute(scores, group, [(i, i ^ span) for i in range(pieces)])]
    all_to_all x1, starting transfers between devices: 5.56 us -> 3.68 us  [expectation(): lax.all_to_all(merged, same_core, split_axis=0, concat_axis=0, tiled=True)]
  transfers between devices with their start and end apart: 14 -> 11, of which waited for: 10 -> 7; matrix products, arithmetic and copies ran while one was open for 2% -> 2% of each run, Pallas kernels for 0% -> 0%
where the time goes in v1:
time: 67.9 us; the launch traced here: 67.5 us
  starting transfers between devices  23.5 us (35%)
  waiting for transfers between devices  18 us (27%)
  blocking collectives  11.7 us (17%)
  Pallas kernels  9.63 us (14%)
  local copies, waits for them, and re-layouts  2.37 us (3%)
  other arithmetic  1.56 us (2%)
  between operations  0.81 us (1%)
    all_to_all x1, blocking collectives, expectation(): lax.all_to_all(scores, group, split_axis=0, concat_axis=0, tiled=True)  11.7 us
    ppermute x7, starting transfers between devices, expectation(): parts[at] = lax.ppermute(parts[at], group, routes_of(steps[at], pieces))  11.2 us
    all_to_all x1, waiting for transfers between devices, expectation(): lax.all_to_all(merged, same_core, split_axis=0, concat_axis=0, tiled=True)  10.1 us
    all_to_all x1, starting transfers between devices, expectation(): lax.all_to_all(refs, same_core, split_axis=0, concat_axis=0, tiled=True)  8.49 us
    pallas_call x1, Pallas kernels, expectation(): pl.pallas_call(functools.partial(prepare_kernel, pixel_count, width, step...  3.94 us
    ppermute x7, waiting for transfers between devices, expectation(): parts[at] = lax.ppermute(parts[at], group, routes_of(steps[at], pieces))  3.77 us
    all_to_all x1, starting transfers between devices, expectation(): lax.all_to_all(merged, same_core, split_axis=0, concat_axis=0, tiled=True)  3.68 us
    pallas_call x1, Pallas kernels, expectation(): pl.pallas_call(functools.partial(score_kernel, rows, route_count, columns...  3.54 us
  transfers between devices with their start and end apart: 11, of which 7 were waited for; matrix products, arithmetic and copies ran while one was open for 2% of the time, Pallas kernels for 0%

profile of v1, /device:TPU:0, one launch (start us, length us, event | category | flops | bytes accessed | tf_op | source)
XLA Modules:
  0.0 67.5 jit_solution(14029594424550017033)
XLA Ops:
  0.6 0.0 copy-start.2
  0.6 0.7 pad_add_fusion.refs_6_.refs_all_12_.place
  1.3 3.9 %prepare.1 = (bf16[16,4,2176]{2,1,0:T(4,128)(2,1)}, bf16[24,2304]{1,0:T(8,128)(2,1)}, bf16[24,2304]{1,0:T(8,128)(2,1)}, bf16[24,2304]{1,0:T(8,128)(2,1)}, bf16[2...) custom-call(bf16[2,33024]{1,0:T(2,128)(2,1)} %bitcast.30, ...), custom_call_target="tpu_custom_call" | custom-call | tf_op jit(solution)/shard_map/prepare/pallas_call | solution.py:360
  5.3 0.0 copy-start
  5.3 8.5 %all-to-all-start = ((bf16[16,4,2176]{2,1,0:T(4,128)(2,1)}), bf16[16,4,2176]{2,1,0:T(4,128)(2,1)S(1)}, u32[]{:S(2)}, u32[]{:S(2)}) async-start(bf16[16,4,2176]{2,1,0:T(4,128)(2,1)} %get-tuple-element.24), calls=%async_computation | async-start | bytes 557056 | tf_op jit(solution)/shard_map/all_to_all | solution.py:374
  13.8 3.7 %collective-permute-start = (bf16[24,2304]{1,0:T(8,128)(2,1)}, bf16[24,2304]{1,0:T(8,128)(2,1)S(1)}, u32[]{:S(2)}, u32[]{:S(2)}) collective-permute-start(bf16[24,2304]{1,0:T(8,128)(2,1)} %get-tuple-element.17), channel_id=1, source_target_pairs={{0,11},{1,10},{2,9},{3,8},{8,3},{9,2},{10,1},{11,0},{4,15},{5,14},... | collective-permute-start | bytes 331784 | tf_op jit(solution)/shard_map/ppermute | solution.py:379
  17.5 0.6 collective-permute-start.1
  18.1 0.6 collective-permute-start.2
  18.6 0.2 collective-permute-start.3
  18.8 2.8 %collective-permute-start.4 = (bf16[24,2304]{1,0:T(8,128)(2,1)}, bf16[24,2304]{1,0:T(8,128)(2,1)S(1)}, u32[]{:S(2)}, u32[]{:S(2)}) collective-permute-start(bf16[24,2304]{1,0:T(8,128)(2,1)} %get-tuple-element.21), channel_id=1, source_target_pairs={{0,3},{1,2},{2,1},{3,0},{8,11},{9,10},{10,9},{11,8},{4,7},{5,6},{6... | collective-permute-start | bytes 331784 | tf_op jit(solution)/shard_map/ppermute | solution.py:379
  21.6 0.1 fusion.3
  21.7 0.5 fusion.7
  22.2 2.5 %all-to-all-done = bf16[16,4,2176]{2,1,0:T(4,128)(2,1)S(1)} async-done(((bf16[16,4,2176]{2,1,0:T(4,128)(2,1)}), bf16[16,4,2176]{2,1,0:T(4,128)(2,1)S(1)}, u32[]{:S(2)}, u32[]{:S(2)}) %all-to-all-start) | async-done | bytes 278560 | tf_op jit(solution)/shard_map/all_to_all | solution.py:374
  24.8 1.0 %collective-permute-done.refs_all_1_ = bf16[24,2304]{1,0:T(8,128)(2,1)S(1)} collective-permute-done((bf16[24,2304]{1,0:T(8,128)(2,1)}, bf16[24,2304]{1,0:T(8,128)(2,1)S(1)}, u32[]{:S(2)}, u32[]{:S(2)}) %collective-permute-start) | collective-permute-done | bytes 110624 | tf_op jit(solution)/shard_map/ppermute | solution.py:379
  25.7 0.7 %collective-permute-start.5 = (bf16[24,2304]{1,0:T(8,128)(2,1)S(1)}, bf16[24,2304]{1,0:T(8,128)(2,1)S(1)}, u32[]{:S(2)}, u32[]{:S(2)}) collective-permute-start(bf16[24,2304]{1,0:T(8,128)(2,1)S(1)} %copy-done.4), channel_id=1, source_target_pairs={{0,9},{1,8},{2,11},{3,10},{8,1},{9,0},{10,3},{11,2},{4,13},{5,12},... | collective-permute-start | bytes 331784 | tf_op jit(solution)/shard_map/ppermute | solution.py:379
  26.4 0.0 collective-permute-done.1.refs_all_2_
  26.4 2.8 %collective-permute-start.6 = (bf16[24,2304]{1,0:T(8,128)(2,1)S(1)}, bf16[24,2304]{1,0:T(8,128)(2,1)S(1)}, u32[]{:S(2)}, u32[]{:S(2)}) collective-permute-start(bf16[24,2304]{1,0:T(8,128)(2,1)S(1)} %copy-done.3), channel_id=1, source_target_pairs={{0,10},{1,11},{2,8},{3,9},{8,2},{9,3},{10,0},{11,1},{4,14},{5,15},... | collective-permute-start | bytes 331784 | tf_op jit(solution)/shard_map/ppermute | solution.py:379
  29.2 0.0 collective-permute-start.7
  29.3 0.5 collective-permute-done.4.refs_all_5_
  29.7 1.6 %collective-permute-done.5.refs_all_6_ = bf16[24,2304]{1,0:T(8,128)(2,1)S(1)} collective-permute-done((bf16[24,2304]{1,0:T(8,128)(2,1)S(1)}, bf16[24,2304]{1,0:T(8,128)(2,1)S(1)}, u32[]{:S(2)}, u32[]{:S(2)}) %collective-permute-start.5) | collective-permute-done | bytes 110624 | tf_op jit(solution)/shard_map/ppermute | solution.py:379
  31.4 0.7 %collective-permute-done.6.refs_all_7_ = bf16[24,2304]{1,0:T(8,128)(2,1)S(1)} collective-permute-done((bf16[24,2304]{1,0:T(8,128)(2,1)S(1)}, bf16[24,2304]{1,0:T(8,128)(2,1)S(1)}, u32[]{:S(2)}, u32[]{:S(2)}) %collective-permute-start.6) | collective-permute-done | bytes 110624 | tf_op jit(solution)/shard_map/ppermute | solution.py:379
  32.1 3.5 %score.1 = (f32[8,24,640]{2,1,0:T(8,128)S(1)}, bf16[8,24,2304]{2,1,0:T(8,128)(2,1)S(1)}) custom-call(bf16[24,2304]{1,0:T(8,128)(2,1)S(1)} %copy-done, bf16[24,2304]{1,0:T(8,128)(2,1)S(1)} %collective-permute-done.refs_all_1_, bf16[24,2304]{1,0:T(8,128)(2,1)S(1)} %collective-permute-done.1.refs_all_2_, ...), custom_call_target="tpu_custom_call" | custom-call | tf_op jit(solution)/shard_map/score/pallas_call | solution.py:392
  35.6 11.7 %all_to_all.15.scores = f32[8,24,640]{2,1,0:T(8,128)S(1)} all-to-all(f32[8,24,640]{2,1,0:T(8,128)S(1)} %get-tuple-element.25), channel_id=1, replica_groups=mesh['groups'=1,'far'=2,'near'=2,'core'=2,'cls'=4] {'near','cls'}, dimensions={0} | all-to-all | bytes 983040 | tf_op jit(solution)/shard_map/all_to_all | solution.py:411
  47.4 2.2 %sums.1 = (f32[4,16,2176]{2,1,0:T(8,128)S(1)}, bf16[4,16,2176]{2,1,0:T(8,128)(2,1)S(1)}, f32[192,128]{1,0:T(8,128)S(1)}) custom-call(f32[8,24,640]{2,1,0:T(8,128)S(1)} %all_to_all.15.scores, bf16[192,2304]{1,0:T(8,128)(2,1)S(1)} %bitcast.26, f32[4,2176]{1,0:T(4,128)S(1)} %reshape.113.refs_all_11_.phases, s32[2]{0:T(128)S(1)} %copy-done.1), custom_call_target="tpu_custom_call" | custom-call | tf_op jit(solution)/shard_map/sums/pallas_call | solution.py:414
  49.5 0.1 collective-permute-start.8
  49.6 1.5 %collective-permute-done.8 = bf16[4,16,2176]{2,1,0:T(8,128)(2,1)S(1)} collective-permute-done((bf16[4,16,2176]{2,1,0:T(8,128)(2,1)S(1)}, bf16[4,16,2176]{2,1,0:T(8,128)(2,1)S(1)}, u32[]{:S(2)}, u32[]{:S(2)}) %collective-permute-start.8) | collective-permute-done | bytes 278560 | tf_op jit(solution)/shard_map/ppermute | solution.py:429
  51.2 0.8 %copy.17 = bf16[16,4,2176]{2,1,0:T(4,128)(2,1)} copy(bf16[16,4,2176]{2,0,1:T(8,128)(2,1)S(1)} %fusion) | data formatting | bytes 557056 | tf_op jit(solution)/shard_map/transpose | solution.py:430
  52.0 3.7 %all-to-all-start.2 = ((bf16[16,4,2176]{2,1,0:T(4,128)(2,1)}), bf16[16,4,2176]{2,1,0:T(4,128)(2,1)S(1)}, u32[]{:S(2)}, u32[]{:S(2)}) async-start(bf16[16,4,2176]{2,1,0:T(4,128)(2,1)} %copy.17), calls=%async_computation.2 | async-start | bytes 557056 | tf_op jit(solution)/shard_map/all_to_all | solution.py:431
  55.7 0.6 dynamic-slice_reduce_fusion
  56.3 10.1 %all-to-all-done.2 = bf16[16,4,2176]{2,1,0:T(4,128)(2,1)S(1)} async-done(((bf16[16,4,2176]{2,1,0:T(4,128)(2,1)}), bf16[16,4,2176]{2,1,0:T(4,128)(2,1)S(1)}, u32[]{:S(2)}, u32[]{:S(2)}) %all-to-all-start.2) | async-done | bytes 278560 | tf_op jit(solution)/shard_map/all_to_all | solution.py:431
  66.5 0.2 reduce_sum.12
  66.8 0.7 %slice.8 = bf16[2,2,16512]{2,0,1:T(2,128)(2,1)} slice(bf16[2,2,17408]{2,0,1:T(2,128)(2,1)S(1)} %reshape.117), slice={[0:2], [0:2], [0:16512]} | slice | bytes 264192 | tf_op jit(solution)/shard_map/slice | solution.py:434
  (18 shorter events, 0.3 us)
Async XLA Ops:
  0.6 20.9 %copy-start.2 = (bf16[8,16512]{1,0:T(8,128)(2,1)S(1)}, bf16[8,16512]{1,0:T(8,128)(2,1)}, u32[]{:S(2)}) copy-start(bf16[8,16512]{1,0:T(8,128)(2,1)} %refs_2_.1) | copy-start | bytes 792580
  5.2 20.5 %copy-start.4 = (bf16[24,2304]{1,0:T(8,128)(2,1)S(1)}, bf16[24,2304]{1,0:T(8,128)(2,1)}, u32[]{:S(2)}) copy-start(bf16[24,2304]{1,0:T(8,128)(2,1)} %get-tuple-element.22) | copy-start | bytes 331780
  5.3 21.2 %copy-start.3 = (bf16[24,2304]{1,0:T(8,128)(2,1)S(1)}, bf16[24,2304]{1,0:T(8,128)(2,1)}, u32[]{:S(2)}) copy-start(bf16[24,2304]{1,0:T(8,128)(2,1)} %get-tuple-element.23) | copy-start | bytes 331780
  5.3 26.8 %copy-start = (bf16[24,2304]{1,0:T(8,128)(2,1)S(1)}, bf16[24,2304]{1,0:T(8,128)(2,1)}, u32[]{:S(2)}) copy-start(bf16[24,2304]{1,0:T(8,128)(2,1)} %get-tuple-element.16.refs_all_0_) | copy-start | bytes 331780
  5.3 26.8 %copy-start.1 = (s32[2]{0:T(128)S(1)}, s32[2]{0:T(128)}, u32[]{:S(2)}) copy-start(s32[2]{0:T(128)} %pad_add_fusion.refs_6_.refs_all_12_.place) | copy-start | bytes 28
  5.3 19.4 %all-to-all-start = ((bf16[16,4,2176]{2,1,0:T(4,128)(2,1)}), bf16[16,4,2176]{2,1,0:T(4,128)(2,1)S(1)}, u32[]{:S(2)}, u32[]{:S(2)}) async-start(bf16[16,4,2176]{2,1,0:T(4,128)(2,1)} %get-tuple-element.24), calls=%async_computation | async-start | bytes 557056 | tf_op jit(solution)/shard_map/all_to_all | solution.py:374
  13.8 11.9 %collective-permute-start = (bf16[24,2304]{1,0:T(8,128)(2,1)}, bf16[24,2304]{1,0:T(8,128)(2,1)S(1)}, u32[]{:S(2)}, u32[]{:S(2)}) collective-permute-start(bf16[24,2304]{1,0:T(8,128)(2,1)} %get-tuple-element.17), channel_id=1, source_target_pairs={{0,11},{1,10},{2,9},{3,8},{8,3},{9,2},{10,1},{11,0},{4,15},{5,14},... | collective-permute-start | bytes 331784 | tf_op jit(solution)/shard_map/ppermute | solution.py:379
  17.5 8.9 %collective-permute-start.1 = (bf16[24,2304]{1,0:T(8,128)(2,1)}, bf16[24,2304]{1,0:T(8,128)(2,1)S(1)}, u32[]{:S(2)}, u32[]{:S(2)}) collective-permute-start(bf16[24,2304]{1,0:T(8,128)(2,1)} %get-tuple-element.18), channel_id=1, source_target_pairs={{0,1},{1,0},{2,3},{3,2},{8,9},{9,8},{10,11},{11,10},{4,5},{5,4},{6... | collective-permute-start | bytes 331784 | tf_op jit(solution)/shard_map/ppermute | solution.py:379
  18.1 11.1 %collective-permute-start.2 = (bf16[24,2304]{1,0:T(8,128)(2,1)}, bf16[24,2304]{1,0:T(8,128)(2,1)S(1)}, u32[]{:S(2)}, u32[]{:S(2)}) collective-permute-start(bf16[24,2304]{1,0:T(8,128)(2,1)} %get-tuple-element.19), channel_id=1, source_target_pairs={{0,2},{1,3},{2,0},{3,1},{8,10},{9,11},{10,8},{11,9},{4,6},{5,7},{6... | collective-permute-start | bytes 331784 | tf_op jit(solution)/shard_map/ppermute | solution.py:379
  18.6 10.6 %collective-permute-start.3 = (bf16[24,2304]{1,0:T(8,128)(2,1)}, bf16[24,2304]{1,0:T(8,128)(2,1)S(1)}, u32[]{:S(2)}, u32[]{:S(2)}) collective-permute-start(bf16[24,2304]{1,0:T(8,128)(2,1)} %get-tuple-element.20), channel_id=1, source_target_pairs={{0,8},{1,9},{2,10},{3,11},{8,0},{9,1},{10,2},{11,3},{4,12},{5,13},... | collective-permute-start | bytes 331784 | tf_op jit(solution)/shard_map/ppermute | solution.py:379
  18.8 10.9 %collective-permute-start.4 = (bf16[24,2304]{1,0:T(8,128)(2,1)}, bf16[24,2304]{1,0:T(8,128)(2,1)S(1)}, u32[]{:S(2)}, u32[]{:S(2)}) collective-permute-start(bf16[24,2304]{1,0:T(8,128)(2,1)} %get-tuple-element.21), channel_id=1, source_target_pairs={{0,3},{1,2},{2,1},{3,0},{8,11},{9,10},{10,9},{11,8},{4,7},{5,6},{6... | collective-permute-start | bytes 331784 | tf_op jit(solution)/shard_map/ppermute | solution.py:379
  25.7 5.6 %collective-permute-start.5 = (bf16[24,2304]{1,0:T(8,128)(2,1)S(1)}, bf16[24,2304]{1,0:T(8,128)(2,1)S(1)}, u32[]{:S(2)}, u32[]{:S(2)}) collective-permute-start(bf16[24,2304]{1,0:T(8,128)(2,1)S(1)} %copy-done.4), channel_id=1, source_target_pairs={{0,9},{1,8},{2,11},{3,10},{8,1},{9,0},{10,3},{11,2},{4,13},{5,12},... | collective-permute-start | bytes 331784 | tf_op jit(solution)/shard_map/ppermute | solution.py:379
  26.4 5.6 %collective-permute-start.6 = (bf16[24,2304]{1,0:T(8,128)(2,1)S(1)}, bf16[24,2304]{1,0:T(8,128)(2,1)S(1)}, u32[]{:S(2)}, u32[]{:S(2)}) collective-permute-start(bf16[24,2304]{1,0:T(8,128)(2,1)S(1)} %copy-done.3), channel_id=1, source_target_pairs={{0,10},{1,11},{2,8},{3,9},{8,2},{9,3},{10,0},{11,1},{4,14},{5,15},... | collective-permute-start | bytes 331784 | tf_op jit(solution)/shard_map/ppermute | solution.py:379
  29.2 2.9 %collective-permute-start.7 = (bf16[16,4,2176]{2,0,1:T(8,128)(2,1)S(1)}, bf16[16,4,2176]{2,0,1:T(8,128)(2,1)S(1)}, u32[]{:S(2)}, u32[]{:S(2)}) collective-permute-start(bf16[16,4,2176]{2,0,1:T(8,128)(2,1)S(1)} %copy.22), channel_id=1, source_target_pairs={{0,4},{4,0},{1,5},{5,1},{2,6},{6,2},{3,7},{7,3},{8,12},{12,8},{9,1... | collective-permute-start | bytes 835592 | tf_op jit(solution)/shard_map/ppermute | solution.py:375
  49.5 1.6 %collective-permute-start.8 = (bf16[4,16,2176]{2,1,0:T(8,128)(2,1)S(1)}, bf16[4,16,2176]{2,1,0:T(8,128)(2,1)S(1)}, u32[]{:S(2)}, u32[]{:S(2)}) collective-permute-start(bf16[4,16,2176]{2,1,0:T(8,128)(2,1)S(1)} %get-tuple-element.29), channel_id=1, source_target_pairs={{0,4},{4,0},{1,5},{5,1},{2,6},{6,2},{3,7},{7,3},{8,12},{12,8},{9,1... | collective-permute-start | bytes 835592 | tf_op jit(solution)/shard_map/ppermute | solution.py:429
  52.0 14.4 %all-to-all-start.2 = ((bf16[16,4,2176]{2,1,0:T(4,128)(2,1)}), bf16[16,4,2176]{2,1,0:T(4,128)(2,1)S(1)}, u32[]{:S(2)}, u32[]{:S(2)}) async-start(bf16[16,4,2176]{2,1,0:T(4,128)(2,1)} %copy.17), calls=%async_computation.2 | async-start | bytes 557056 | tf_op jit(solution)/shard_map/all_to_all | solution.py:431

commit v2 on v1

--- a/solution.py
+++ b/solution.py
@@ -79,9 +79,9 @@
                     )
 
 
-def prepare_kernel(pixel_count, width, steps, *refs):
-    distant, (place, split), rest = refs[:6], refs[6:8], refs[8:]
-    outs, near, (ctf_rows, whole, table, arrived) = rest[: len(steps)], rest[len(steps) : -4], rest[-4:]
+def prepare_kernel(pixel_count, width, steps, group, *refs):
+    distant, (split, *outs), rest = refs[:6], refs[6 : 7 + len(steps)], refs[7 + len(steps) :]
+    near, (split_here, whole, ctf_rows, table, arrived, left) = rest[:6], rest[6:]
     copies = [
         pltpu.make_async_copy(far, here, arrived.at[i])
         for i, (far, here) in enumerate(zip(distant, near))
@@ -89,17 +89,26 @@
     for copy in copies:
         copy.start()
     copies[0].wait()
-    split_refs(pixel_count, width, near[0], split)
-    for copy in copies[1:]:
+    split_refs(pixel_count, width, near[0], split_here)
+    sent = [pltpu.make_async_copy(split_here, split, left.at[0])]
+    sent[0].start()
+    for copy in copies[2:]:
         copy.wait()
-    align(pixel_count, width, steps, *near[1:], place, outs, ctf_rows, whole, table)
+    align(pixel_count, width, *near[1:], whole, ctf_rows, table, copies[1])
+    place = lax.axis_index(group)
+    for step, out in zip(steps, outs):
+        piece = whole.at[other(place, step, len(steps))]
+        sent.append(pltpu.make_async_copy(piece, out, left.at[len(sent)]))
+        sent[-1].start()
+    for copy in sent:
+        copy.wait()
 
 
 def align(
-    pixel_count, width, steps, images, ctf, groups, offsets, routes, place, outs, ctf_rows, whole, table
+    pixel_count, width, images, ctf, groups, offsets, routes, whole, ctf_rows, table, coming
 ):
     rows = images.shape[0]
-    pieces = len(outs)
+    pieces = whole.shape[0]
     route_count = routes.shape[0]
     table[...] = jnp.zeros(table.shape, f32)
     table[0:2, 0:rows] = offsets[...].astype(f32)
@@ -124,6 +133,7 @@
     blocks = -(-pixel_count // block)
     start = lax.broadcasted_iota(jnp.int32, (rows, blocks), 1) * (block // KY)
     start_cos, start_sin = unit_circle(start.astype(f32) * shift_across)
+    coming.wait()
     for piece in range(pieces):
         for part in range(width // LANES):
             low = piece * width + part * LANES
@@ -149,9 +159,8 @@
     for r in range(route_count):
         notes = jnp.where(lane == r, facts[:, 3 + r : 4 + r], notes)
     notes = jnp.concatenate([notes, notes], axis=0).astype(bf16)
-    for step, out in zip(steps, outs):
-        out[:, 0:width] = whole[other(place[0], step, pieces)]
-        out[:, width : width + LANES] = notes
+    for piece in range(pieces):
+        whole[piece, :, width : width + LANES] = notes
 
 
 def lane_facts(total, owners, same_core, columns, core_here):
@@ -169,27 +178,24 @@
     return jnp.where(row == spot, 1.0, 0.0).astype(bf16)
 
 
-def score_kernel(rows, route_count, columns, steps, *refs_all):
-    count = len(steps)
-    parts = refs_all[:count]
-    *blocks, ctf, phases, place, out, aligned, turned, power, dense, notes, packed = (
-        refs_all[count:]
-    )
-    same_core = blocks[0].shape[1]
-    owners = len(blocks) * same_core
+def block_facts(held, peers, blocks, columns, core_here):
+    each = SHIFTS * held * peers
+    lane = lax.broadcasted_iota(jnp.int32, (1, each * blocks), 1)
+    inside, peer = lax.rem(lane, each), lax.rem(lane, peers)
+    core = source(core_here, lane // each, blocks)
+    direction = (peer // columns) * blocks + core
+    spot = (inside // peers) * columns + lax.rem(peer, columns)
+    return direction.astype(f32), spot.astype(f32)
+
+
+def turn_kernel(refs, ctf, phases, turned, energy, power):
     width = phases.shape[1]
-    held = blocks[0].shape[0] // 2
-    total = held * len(blocks) * blocks[0].shape[1]
-    for step, part in zip(steps, parts):
-        aligned[source(place[0], step, count)] = part[...]
+    held = refs.shape[0] // 2
+    total = held * refs.shape[1]
     for low in range(0, width, LANES):
         here = slice(low, low + LANES)
-        real = jnp.concatenate(
-            [block[k, :, here] for k in range(held) for block in blocks], axis=0
-        )
-        imag = jnp.concatenate(
-            [block[held + k, :, here] for k in range(held) for block in blocks], axis=0
-        )
+        real = jnp.concatenate([refs[k, :, here] for k in range(held)], axis=0)
+        imag = jnp.concatenate([refs[held + k, :, here] for k in range(held)], axis=0)
         turned[0, 0:total, here] = real
         turned[1, 0:total, here] = imag
         real, imag = real.astype(f32), imag.astype(f32)
@@ -204,23 +210,42 @@
             at = at + total
             turned[0, at : at + total, here] = (rc + is_).astype(bf16)
             turned[1, at : at + total, here] = (ic - rs).astype(bf16)
+    table = ctf[...].astype(f32)
+    half = 0.5 * lax.dot_general(
+        table * table,
+        power[...],
+        (((1,), (1,)), ((), ())),
+        precision=highest,
+        preferred_element_type=f32,
+    )
+    energy[...] = jnp.concatenate([half] * SHIFTS, axis=1)
+
+
+def score_kernel(rows, route_count, columns, held, cores, steps, *refs_all):
+    count = len(steps)
+    parts, blocks, energies = refs_all[:count], refs_all[count:][:cores], refs_all[count + cores :][:cores]
+    place, out, aligned, dense, notes, packed = refs_all[count + 2 * cores :]
+    width = blocks[0].shape[2]
+    each = blocks[0].shape[1]
+    for step, part in zip(steps, parts):
+        aligned[source(place[0], step, count)] = part[...]
     across = (((1,), (1,)), ((), ()))
     images = aligned[:, :, 0:width].reshape(2 * rows * count, width)
-    real = lax.dot_general(images, turned[0], across, preferred_element_type=f32)
-    imag = lax.dot_general(images, turned[1], across, preferred_element_type=f32)
-    table = ctf[...].astype(f32)
-    energy = lax.dot_general(
-        table * table, power[...], across, precision=highest, preferred_element_type=f32
-    )
-    energy = jnp.concatenate([energy] * SHIFTS, axis=1) * 0.5
+    for block, turned in enumerate(blocks):
+        real = lax.dot_general(images, turned[0], across, preferred_element_type=f32)
+        imag = lax.dot_general(images, turned[1], across, preferred_element_type=f32)
+        for at in range(count):
+            low = 2 * rows * at
+            dense[at * rows : (at + 1) * rows, block * each : (block + 1) * each] = (
+                real[low : low + rows, :] + imag[low + rows : low + 2 * rows, :]
+            )
     for at in range(count):
-        low = 2 * rows * at
         mine = slice(at * rows, (at + 1) * rows)
-        dense[mine, :] = real[low : low + rows, :] + imag[low + rows : low + 2 * rows, :]
         notes[mine, :] = aligned[at, 0:rows, width : width + LANES].astype(f32)
+    energy = jnp.concatenate([energy[...] for energy in energies], axis=1)
     facts = notes[...]
     values = dense[...]
-    for g in range(table.shape[0]):
+    for g in range(energy.shape[0]):
         values = values - jnp.where(
             facts[:, route_count : route_count + 1] == float(g), energy[g : g + 1, :], 0.0
         )
@@ -229,7 +254,7 @@
     second = rest.astype(bf16)
     third = (rest - second.astype(f32)).astype(bf16)
     terms = [first.astype(f32), second.astype(f32), third.astype(f32)]
-    direction, spot = lane_facts(total, owners, same_core, columns, place[1])
+    direction, spot = block_facts(held, each // (SHIFTS * held), cores, columns, place[1])
     spots = SHIFTS * held * columns
     particles = rows * count
     stacked = []
@@ -356,21 +381,26 @@
         offsets.T,
         routes.T,
     )
+    split = jax.ShapeDtypeStruct((peers, 2 * held, width), bf16)
     piece = jax.ShapeDtypeStruct((2 * rows, width + LANES), bf16)
+    in_place = pl.BlockSpec(memory_space=pltpu.HBM)
     refs, *parts = pl.pallas_call(
-        functools.partial(prepare_kernel, pixel_count, width, steps),
-        out_shape=[jax.ShapeDtypeStruct((peers, 2 * held, width), bf16)] + [piece] * pieces,
-        in_specs=[pl.BlockSpec(memory_space=pltpu.HBM)] * len(distant) + [scalars],
+        functools.partial(prepare_kernel, pixel_count, width, steps, group),
+        out_shape=[split] + [piece] * pieces,
+        in_specs=[in_place] * len(distant),
+        out_specs=[in_place] * (1 + pieces),
         scratch_shapes=[pltpu.VMEM(array.shape, array.dtype) for array in distant]
         + [
+            pltpu.VMEM(split.shape, bf16),
+            pltpu.VMEM((pieces, 2 * rows, width + LANES), bf16),
             pltpu.VMEM((rows, pixel_count), f32),
-            pltpu.VMEM((pieces, 2 * rows, width), bf16),
             pltpu.VMEM((-(-(3 + route_count) // 8) * 8, -(-rows // LANES) * LANES), f32),
             pltpu.SemaphoreType.DMA((len(distant),)),
+            pltpu.SemaphoreType.DMA((1 + pieces,)),
         ],
         compiler_params=pltpu.CompilerParams(vmem_limit_bytes=60 << 20),
         name="prepare",
-    )(*distant, where)
+    )(*distant)
     refs = lax.all_to_all(refs, same_core, split_axis=0, concat_axis=0, tiled=True)
     blocks = [refs] + [lax.ppermute(refs, "core", routes_of(step, cores)) for step in range(1, cores)]
     blocks = [block.transpose(1, 0, 2) for block in blocks]
@@ -389,23 +419,35 @@
     count = pieces * rows
     listings = route_count * SHIFTS * held * columns
     folds = 4 if count % 32 == 0 else 1
+    turned, energies = zip(
+        *(
+            pl.pallas_call(
+                turn_kernel,
+                out_shape=(
+                    jax.ShapeDtypeStruct((2, SHIFTS * held * peers, width), bf16),
+                    jax.ShapeDtypeStruct((ctf.shape[0], SHIFTS * held * peers), f32),
+                ),
+                scratch_shapes=[pltpu.VMEM((held * peers, width), f32)],
+                compiler_params=params,
+            )(block, ctf_here, phases)
+            for block in blocks
+        )
+    )
     scores, aligned = pl.pallas_call(
-        functools.partial(score_kernel, rows, route_count, columns, steps),
+        functools.partial(score_kernel, rows, route_count, columns, held, cores, steps),
         out_shape=(
             jax.ShapeDtypeStruct((pieces, count // folds, folds * listings), f32),
             jax.ShapeDtypeStruct((pieces, 2 * rows, width + LANES), bf16),
         ),
-        in_specs=[vectors] * (pieces + cores + 2) + [scalars],
+        in_specs=[vectors] * (pieces + 2 * cores) + [scalars],
         scratch_shapes=[
-            pltpu.VMEM((2, SHIFTS * total, width), bf16),
-            pltpu.VMEM((total, width), f32),
             pltpu.VMEM((count, SHIFTS * total), f32),
             pltpu.VMEM((count, LANES), f32),
             pltpu.VMEM((count // folds, folds * listings), f32),
         ],
         compiler_params=params,
         name="score",
-    )(*parts, *blocks, ctf_here, phases, where)
+    )(*parts, *turned, *energies, where)
     aligned = aligned.reshape(pieces * 2 * rows, width + LANES)
 
     scores = lax.all_to_all(scores, group, split_axis=0, concat_axis=0, tiled=True)

time: 67.9 us -> 67.9 us (level)
  waiting for transfers between devices: 18 us -> 21.3 us
  starting transfers between devices: 23.5 us -> 21.6 us
    all_to_all x1, waiting for transfers between devices: 2.53 us -> 5.2 us  [expectation(): lax.all_to_all(refs, same_core, split_axis=0, concat_axis=0, tiled=True)]
    ppermute x7, starting transfers between devices: 11.2 us -> 9.41 us  [expectation(): parts[at] = lax.ppermute(parts[at], group, routes_of(steps[at], pieces))]
    pallas_call x0 -> x2, Pallas kernels: none -> 1.22 us  [expectation(): pl.pallas_call(turn_kernel, out_shape=(jax.ShapeDtypeStruct((2, SHIFTS *...]
    pallas_call x1, Pallas kernels: 3.54 us -> 2.32 us  [expectation(): pl.pallas_call(functools.partial(score_kernel, rows, route_count, columns...]
  transfers between devices with their start and end apart: 11 -> 11, of which waited for: 7 -> 6; matrix products, arithmetic and copies ran while one was open for 2% -> 2% of each run, Pallas kernels for 0% -> 2%
where the time goes in v2:
time: 67.9 us; the launch traced here: 67.5 us
  starting transfers between devices  21.6 us (32%)
  waiting for transfers between devices  21.3 us (31%)
  blocking collectives  11.2 us (16%)
  Pallas kernels  9.29 us (14%)
  local copies, waits for them, and re-layouts  2.36 us (3%)
  other arithmetic  0.98 us (1%)
  between operations  0.82 us (1%)
    all_to_all x1, blocking collectives, expectation(): lax.all_to_all(scores, group, split_axis=0, concat_axis=0, tiled=True)  11.2 us
    all_to_all x1, waiting for transfers between devices, expectation(): lax.all_to_all(merged, same_core, split_axis=0, concat_axis=0, tiled=True)  10.3 us
    ppermute x7, starting transfers between devices, expectation(): parts[at] = lax.ppermute(parts[at], group, routes_of(steps[at], pieces))  9.41 us
    all_to_all x1, starting transfers between devices, expectation(): lax.all_to_all(refs, same_core, split_axis=0, concat_axis=0, tiled=True)  8.49 us
    all_to_all x1, waiting for transfers between devices, expectation(): lax.all_to_all(refs, same_core, split_axis=0, concat_axis=0, tiled=True)  5.2 us
    ppermute x7, waiting for transfers between devices, expectation(): parts[at] = lax.ppermute(parts[at], group, routes_of(steps[at], pieces))  4.33 us
    pallas_call x1, Pallas kernels, expectation(): pl.pallas_call(functools.partial(prepare_kernel, pixel_count, width, step...  3.58 us
    all_to_all x1, starting transfers between devices, expectation(): lax.all_to_all(merged, same_core, split_axis=0, concat_axis=0, tiled=True)  3.53 us
  transfers between devices with their start and end apart: 11, of which 6 were waited for; matrix products, arithmetic and copies ran while one was open for 2% of the time, Pallas kernels for 2%

profile of v2, /device:TPU:0, one launch (start us, length us, event | category | flops | bytes accessed | tf_op | source)
XLA Modules:
  0.0 67.5 jit_solution(17031837364436815513)
XLA Ops:
  0.6 3.6 %prepare.1 = (bf16[16,4,2176]{2,1,0:T(4,128)(2,1)}, bf16[24,2304]{1,0:T(8,128)(2,1)}, bf16[24,2304]{1,0:T(8,128)(2,1)}, bf16[24,2304]{1,0:T(8,128)(2,1)}, bf16[2...) custom-call(bf16[2,33024]{1,0:T(2,128)(2,1)} %bitcast.30, ...), custom_call_target="tpu_custom_call" | custom-call | tf_op jit(solution)/shard_map/prepare/pallas_call | solution.py:387
  4.3 0.0 copy-start
  4.3 8.5 %all-to-all-start = ((bf16[16,4,2176]{2,1,0:T(4,128)(2,1)}), bf16[16,4,2176]{2,1,0:T(4,128)(2,1)S(1)}, u32[]{:S(2)}, u32[]{:S(2)}) async-start(bf16[16,4,2176]{2,1,0:T(4,128)(2,1)} %get-tuple-element.28), calls=%async_computation | async-start | bytes 557056 | tf_op jit(solution)/shard_map/all_to_all | solution.py:404
  12.8 3.7 %collective-permute-start = (bf16[24,2304]{1,0:T(8,128)(2,1)}, bf16[24,2304]{1,0:T(8,128)(2,1)S(1)}, u32[]{:S(2)}, u32[]{:S(2)}) collective-permute-start(bf16[24,2304]{1,0:T(8,128)(2,1)} %get-tuple-element.21), channel_id=1, source_target_pairs={{0,11},{1,10},{2,9},{3,8},{8,3},{9,2},{10,1},{11,0},{4,15},{5,14},... | collective-permute-start | bytes 331784 | tf_op jit(solution)/shard_map/ppermute | solution.py:409
  16.5 0.6 collective-permute-start.1
  17.1 0.6 collective-permute-start.2
  17.6 0.2 collective-permute-start.3
  17.8 0.1 fusion.3
  17.9 0.5 fusion.7
  18.4 5.2 %all-to-all-done = bf16[16,4,2176]{2,1,0:T(4,128)(2,1)S(1)} async-done(((bf16[16,4,2176]{2,1,0:T(4,128)(2,1)}), bf16[16,4,2176]{2,1,0:T(4,128)(2,1)S(1)}, u32[]{:S(2)}, u32[]{:S(2)}) %all-to-all-start) | async-done | bytes 278560 | tf_op jit(solution)/shard_map/all_to_all | solution.py:404
  23.6 0.1 collective-permute-start.7
  23.8 0.9 %collective-permute-done.refs_all_1_ = bf16[24,2304]{1,0:T(8,128)(2,1)S(1)} collective-permute-done((bf16[24,2304]{1,0:T(8,128)(2,1)}, bf16[24,2304]{1,0:T(8,128)(2,1)S(1)}, u32[]{:S(2)}, u32[]{:S(2)}) %collective-permute-start) | collective-permute-done | bytes 110624 | tf_op jit(solution)/shard_map/ppermute | solution.py:409
  24.7 0.2 collective-permute-start.4
  24.9 1.9 %collective-permute-start.5 = (bf16[24,2304]{1,0:T(8,128)(2,1)S(1)}, bf16[24,2304]{1,0:T(8,128)(2,1)S(1)}, u32[]{:S(2)}, u32[]{:S(2)}) collective-permute-start(bf16[24,2304]{1,0:T(8,128)(2,1)S(1)} %copy-done.3), channel_id=1, source_target_pairs={{0,9},{1,8},{2,11},{3,10},{8,1},{9,0},{10,3},{11,2},{4,13},{5,12},... | collective-permute-start | bytes 331784 | tf_op jit(solution)/shard_map/ppermute | solution.py:409
  26.9 2.2 %collective-permute-start.6 = (bf16[24,2304]{1,0:T(8,128)(2,1)S(1)}, bf16[24,2304]{1,0:T(8,128)(2,1)S(1)}, u32[]{:S(2)}, u32[]{:S(2)}) collective-permute-start(bf16[24,2304]{1,0:T(8,128)(2,1)S(1)} %copy-done.2), channel_id=1, source_target_pairs={{0,10},{1,11},{2,8},{3,9},{8,2},{9,3},{10,0},{11,1},{4,14},{5,15},... | collective-permute-start | bytes 331784 | tf_op jit(solution)/shard_map/ppermute | solution.py:409
  29.1 0.1 pad_add_fusion.refs_all_12_.place
  29.2 0.6 shard_map.77
  29.8 0.6 shard_map.78
  30.4 1.9 %collective-permute-done.4.refs_all_5_ = bf16[24,2304]{1,0:T(8,128)(2,1)S(1)} collective-permute-done((bf16[24,2304]{1,0:T(8,128)(2,1)S(1)}, bf16[24,2304]{1,0:T(8,128)(2,1)S(1)}, u32[]{:S(2)}, u32[]{:S(2)}) %collective-permute-start.4) | collective-permute-done | bytes 110624 | tf_op jit(solution)/shard_map/ppermute | solution.py:409
  32.3 1.6 %collective-permute-done.6.refs_all_7_ = bf16[24,2304]{1,0:T(8,128)(2,1)S(1)} collective-permute-done((bf16[24,2304]{1,0:T(8,128)(2,1)S(1)}, bf16[24,2304]{1,0:T(8,128)(2,1)S(1)}, u32[]{:S(2)}, u32[]{:S(2)}) %collective-permute-start.6) | collective-permute-done | bytes 110624 | tf_op jit(solution)/shard_map/ppermute | solution.py:409
  33.9 2.3 %score.1 = (f32[8,24,640]{2,1,0:T(8,128)S(1)}, bf16[8,24,2304]{2,1,0:T(8,128)(2,1)S(1)}) custom-call(bf16[24,2304]{1,0:T(8,128)(2,1)S(1)} %copy-done, bf16[24,2304]{1,0:T(8,128)(2,1)S(1)} %collective-permute-done.refs_all_1_, bf16[24,2304]{1,0:T(8,128)(2,1)S(1)} %collective-permute-done.1.refs_all_2_, ...), custom_call_target="tpu_custom_call" | custom-call | tf_op jit(solution)/shard_map/score/pallas_call | solution.py:436
  36.2 11.2 %all_to_all.15.scores = f32[8,24,640]{2,1,0:T(8,128)S(1)} all-to-all(f32[8,24,640]{2,1,0:T(8,128)S(1)} %get-tuple-element.33), channel_id=1, replica_groups=mesh['groups'=1,'far'=2,'near'=2,'core'=2,'cls'=4] {'near','cls'}, dimensions={0} | all-to-all | bytes 983040 | tf_op jit(solution)/shard_map/all_to_all | solution.py:453
  47.4 2.2 %sums.1 = (f32[4,16,2176]{2,1,0:T(8,128)S(1)}, bf16[4,16,2176]{2,1,0:T(8,128)(2,1)S(1)}, f32[192,128]{1,0:T(8,128)S(1)}) custom-call(f32[8,24,640]{2,1,0:T(8,128)S(1)} %all_to_all.15.scores, bf16[192,2304]{1,0:T(8,128)(2,1)S(1)} %bitcast.26, f32[4,2176]{1,0:T(4,128)S(1)} %reshape.113.phases, s32[2]{0:T(128)S(1)} %pad_add_fusion.refs_all_12_.place), custom_call_target="tpu_custom_call" | custom-call | tf_op jit(solution)/shard_map/sums/pallas_call | solution.py:456
  49.5 0.1 collective-permute-start.8
  49.6 1.5 %collective-permute-done.8 = bf16[4,16,2176]{2,1,0:T(8,128)(2,1)S(1)} collective-permute-done((bf16[4,16,2176]{2,1,0:T(8,128)(2,1)S(1)}, bf16[4,16,2176]{2,1,0:T(8,128)(2,1)S(1)}, u32[]{:S(2)}, u32[]{:S(2)}) %collective-permute-start.8) | collective-permute-done | bytes 278560 | tf_op jit(solution)/shard_map/ppermute | solution.py:471
  51.2 0.1 fusion
  51.2 0.8 %copy.17 = bf16[16,4,2176]{2,1,0:T(4,128)(2,1)} copy(bf16[16,4,2176]{2,0,1:T(8,128)(2,1)S(1)} %fusion) | data formatting | bytes 557056 | tf_op jit(solution)/shard_map/transpose | solution.py:472
  52.0 3.5 %all-to-all-start.2 = ((bf16[16,4,2176]{2,1,0:T(4,128)(2,1)}), bf16[16,4,2176]{2,1,0:T(4,128)(2,1)S(1)}, u32[]{:S(2)}, u32[]{:S(2)}) async-start(bf16[16,4,2176]{2,1,0:T(4,128)(2,1)} %copy.17), calls=%async_computation.2 | async-start | bytes 557056 | tf_op jit(solution)/shard_map/all_to_all | solution.py:473
  55.6 0.6 dynamic-slice_reduce_fusion
  56.2 10.3 %all-to-all-done.2 = bf16[16,4,2176]{2,1,0:T(4,128)(2,1)S(1)} async-done(((bf16[16,4,2176]{2,1,0:T(4,128)(2,1)}), bf16[16,4,2176]{2,1,0:T(4,128)(2,1)S(1)}, u32[]{:S(2)}, u32[]{:S(2)}) %all-to-all-start.2) | async-done | bytes 278560 | tf_op jit(solution)/shard_map/all_to_all | solution.py:473
  66.5 0.2 reduce_sum.12
  66.8 0.7 %slice.8 = bf16[2,2,16512]{2,0,1:T(2,128)(2,1)} slice(bf16[2,2,17408]{2,0,1:T(2,128)(2,1)S(1)} %reshape.117), slice={[0:2], [0:2], [0:16512]} | slice | bytes 264192 | tf_op jit(solution)/shard_map/slice | solution.py:476
  (20 shorter events, 0.2 us)
Async XLA Ops:
  0.6 17.2 %copy-start.1 = (bf16[8,16512]{1,0:T(8,128)(2,1)S(1)}, bf16[8,16512]{1,0:T(8,128)(2,1)}, u32[]{:S(2)}) copy-start(bf16[8,16512]{1,0:T(8,128)(2,1)} %refs_2_.1) | copy-start | bytes 792580
  4.2 20.5 %copy-start.4 = (bf16[24,2304]{1,0:T(8,128)(2,1)S(1)}, bf16[24,2304]{1,0:T(8,128)(2,1)}, u32[]{:S(2)}) copy-start(bf16[24,2304]{1,0:T(8,128)(2,1)} %get-tuple-element.25) | copy-start | bytes 331780
  4.2 20.7 %copy-start.3 = (bf16[24,2304]{1,0:T(8,128)(2,1)S(1)}, bf16[24,2304]{1,0:T(8,128)(2,1)}, u32[]{:S(2)}) copy-start(bf16[24,2304]{1,0:T(8,128)(2,1)} %get-tuple-element.26) | copy-start | bytes 331780
  4.2 22.6 %copy-start.2 = (bf16[24,2304]{1,0:T(8,128)(2,1)S(1)}, bf16[24,2304]{1,0:T(8,128)(2,1)}, u32[]{:S(2)}) copy-start(bf16[24,2304]{1,0:T(8,128)(2,1)} %get-tuple-element.27) | copy-start | bytes 331780
  4.3 29.6 %copy-start = (bf16[24,2304]{1,0:T(8,128)(2,1)S(1)}, bf16[24,2304]{1,0:T(8,128)(2,1)}, u32[]{:S(2)}) copy-start(bf16[24,2304]{1,0:T(8,128)(2,1)} %get-tuple-element.20.refs_all_0_) | copy-start | bytes 331780
  4.3 19.3 %all-to-all-start = ((bf16[16,4,2176]{2,1,0:T(4,128)(2,1)}), bf16[16,4,2176]{2,1,0:T(4,128)(2,1)S(1)}, u32[]{:S(2)}, u32[]{:S(2)}) async-start(bf16[16,4,2176]{2,1,0:T(4,128)(2,1)} %get-tuple-element.28), calls=%async_computation | async-start | bytes 557056 | tf_op jit(solution)/shard_map/all_to_all | solution.py:404
  12.8 11.9 %collective-permute-start = (bf16[24,2304]{1,0:T(8,128)(2,1)}, bf16[24,2304]{1,0:T(8,128)(2,1)S(1)}, u32[]{:S(2)}, u32[]{:S(2)}) collective-permute-start(bf16[24,2304]{1,0:T(8,128)(2,1)} %get-tuple-element.21), channel_id=1, source_target_pairs={{0,11},{1,10},{2,9},{3,8},{8,3},{9,2},{10,1},{11,0},{4,15},{5,14},... | collective-permute-start | bytes 331784 | tf_op jit(solution)/shard_map/ppermute | solution.py:409
  16.5 8.5 %collective-permute-start.1 = (bf16[24,2304]{1,0:T(8,128)(2,1)}, bf16[24,2304]{1,0:T(8,128)(2,1)S(1)}, u32[]{:S(2)}, u32[]{:S(2)}) collective-permute-start(bf16[24,2304]{1,0:T(8,128)(2,1)} %get-tuple-element.22), channel_id=1, source_target_pairs={{0,1},{1,0},{2,3},{3,2},{8,9},{9,8},{10,11},{11,10},{4,5},{5,4},{6... | collective-permute-start | bytes 331784 | tf_op jit(solution)/shard_map/ppermute | solution.py:409
  17.1 13.4 %collective-permute-start.2 = (bf16[24,2304]{1,0:T(8,128)(2,1)}, bf16[24,2304]{1,0:T(8,128)(2,1)S(1)}, u32[]{:S(2)}, u32[]{:S(2)}) collective-permute-start(bf16[24,2304]{1,0:T(8,128)(2,1)} %get-tuple-element.23), channel_id=1, source_target_pairs={{0,2},{1,3},{2,0},{3,1},{8,10},{9,11},{10,8},{11,9},{4,6},{5,7},{6... | collective-permute-start | bytes 331784 | tf_op jit(solution)/shard_map/ppermute | solution.py:409
  17.6 12.8 %collective-permute-start.3 = (bf16[24,2304]{1,0:T(8,128)(2,1)}, bf16[24,2304]{1,0:T(8,128)(2,1)S(1)}, u32[]{:S(2)}, u32[]{:S(2)}) collective-permute-start(bf16[24,2304]{1,0:T(8,128)(2,1)} %get-tuple-element.24), channel_id=1, source_target_pairs={{0,8},{1,9},{2,10},{3,11},{8,0},{9,1},{10,2},{11,3},{4,12},{5,13},... | collective-permute-start | bytes 331784 | tf_op jit(solution)/shard_map/ppermute | solution.py:409
  23.6 3.2 %collective-permute-start.7 = (bf16[16,4,2176]{2,0,1:T(8,128)(2,1)S(1)}, bf16[16,4,2176]{2,0,1:T(8,128)(2,1)S(1)}, u32[]{:S(2)}, u32[]{:S(2)}) collective-permute-start(bf16[16,4,2176]{2,0,1:T(8,128)(2,1)S(1)} %copy.22), channel_id=1, source_target_pairs={{0,4},{4,0},{1,5},{5,1},{2,6},{6,2},{3,7},{7,3},{8,12},{12,8},{9,1... | collective-permute-start | bytes 835592 | tf_op jit(solution)/shard_map/ppermute | solution.py:405
  24.7 7.6 %collective-permute-start.4 = (bf16[24,2304]{1,0:T(8,128)(2,1)S(1)}, bf16[24,2304]{1,0:T(8,128)(2,1)S(1)}, u32[]{:S(2)}, u32[]{:S(2)}) collective-permute-start(bf16[24,2304]{1,0:T(8,128)(2,1)S(1)} %copy-done.4), channel_id=1, source_target_pairs={{0,3},{1,2},{2,1},{3,0},{8,11},{9,10},{10,9},{11,8},{4,7},{5,6},{6... | collective-permute-start | bytes 331784 | tf_op jit(solution)/shard_map/ppermute | solution.py:409
  24.9 7.3 %collective-permute-start.5 = (bf16[24,2304]{1,0:T(8,128)(2,1)S(1)}, bf16[24,2304]{1,0:T(8,128)(2,1)S(1)}, u32[]{:S(2)}, u32[]{:S(2)}) collective-permute-start(bf16[24,2304]{1,0:T(8,128)(2,1)S(1)} %copy-done.3), channel_id=1, source_target_pairs={{0,9},{1,8},{2,11},{3,10},{8,1},{9,0},{10,3},{11,2},{4,13},{5,12},... | collective-permute-start | bytes 331784 | tf_op jit(solution)/shard_map/ppermute | solution.py:409
  26.9 7.0 %collective-permute-start.6 = (bf16[24,2304]{1,0:T(8,128)(2,1)S(1)}, bf16[24,2304]{1,0:T(8,128)(2,1)S(1)}, u32[]{:S(2)}, u32[]{:S(2)}) collective-permute-start(bf16[24,2304]{1,0:T(8,128)(2,1)S(1)} %copy-done.2), channel_id=1, source_target_pairs={{0,10},{1,11},{2,8},{3,9},{8,2},{9,3},{10,0},{11,1},{4,14},{5,15},... | collective-permute-start | bytes 331784 | tf_op jit(solution)/shard_map/ppermute | solution.py:409
  49.5 1.6 %collective-permute-start.8 = (bf16[4,16,2176]{2,1,0:T(8,128)(2,1)S(1)}, bf16[4,16,2176]{2,1,0:T(8,128)(2,1)S(1)}, u32[]{:S(2)}, u32[]{:S(2)}) collective-permute-start(bf16[4,16,2176]{2,1,0:T(8,128)(2,1)S(1)} %get-tuple-element.37), channel_id=1, source_target_pairs={{0,4},{4,0},{1,5},{5,1},{2,6},{6,2},{3,7},{7,3},{8,12},{12,8},{9,1... | collective-permute-start | bytes 835592 | tf_op jit(solution)/shard_map/ppermute | solution.py:471
  52.0 14.4 %all-to-all-start.2 = ((bf16[16,4,2176]{2,1,0:T(4,128)(2,1)}), bf16[16,4,2176]{2,1,0:T(4,128)(2,1)S(1)}, u32[]{:S(2)}, u32[]{:S(2)}) async-start(bf16[16,4,2176]{2,1,0:T(4,128)(2,1)} %copy.17), calls=%async_computation.2 | async-start | bytes 557056 | tf_op jit(solution)/shard_map/all_to_all | solution.py:473

commit v3 on v2

--- a/solution.py
+++ b/solution.py
@@ -163,16 +163,6 @@
         whole[piece, :, width : width + LANES] = notes
 
 
-def lane_facts(total, owners, same_core, columns, core_here):
-    lane = lax.broadcasted_iota(jnp.int32, (1, SHIFTS * total), 1)
-    owner = lax.rem(lane, owners)
-    core = source(core_here, owner // same_core, owners // same_core)
-    direction = (lax.rem(owner, same_core) // columns) * (owners // same_core) + core
-    shift, held = lane // total, lax.rem(lane, total) // owners
-    spot = (shift * (total // owners) + held) * columns + lax.rem(owner, columns)
-    return direction.astype(f32), spot.astype(f32)
-
-
 def spot_table(spot, spots):
     row = lax.broadcasted_iota(jnp.int32, (spots, spot.shape[1]), 0).astype(f32)
     return jnp.where(row == spot, 1.0, 0.0).astype(bf16)
@@ -224,11 +214,12 @@
 def score_kernel(rows, route_count, columns, held, cores, steps, *refs_all):
     count = len(steps)
     parts, blocks, energies = refs_all[:count], refs_all[count:][:cores], refs_all[count + cores :][:cores]
-    place, out, aligned, dense, notes, packed = refs_all[count + 2 * cores :]
+    out, aligned, dense, notes, packed = refs_all[count + 2 * cores :]
+    place, core = lax.axis_index(("near", "cls")), lax.axis_index("core")
     width = blocks[0].shape[2]
     each = blocks[0].shape[1]
     for step, part in zip(steps, parts):
-        aligned[source(place[0], step, count)] = part[...]
+        aligned[source(place, step, count)] = part[...]
     across = (((1,), (1,)), ((), ()))
     images = aligned[:, :, 0:width].reshape(2 * rows * count, width)
     for block, turned in enumerate(blocks):
@@ -254,7 +245,7 @@
     second = rest.astype(bf16)
     third = (rest - second.astype(f32)).astype(bf16)
     terms = [first.astype(f32), second.astype(f32), third.astype(f32)]
-    direction, spot = block_facts(held, each // (SHIFTS * held), cores, columns, place[1])
+    direction, spot = block_facts(held, each // (SHIFTS * held), cores, columns, core)
     spots = SHIFTS * held * columns
     particles = rows * count
     stacked = []
@@ -280,15 +271,38 @@
         out[copy] = packed[...]
 
 
-def sums_kernel(rows, route_count, columns, scores, aligned, phases, place, *outs_and_scratch):
-    *outs, evidence, tall, wide = outs_and_scratch
+def turn_back(weights_real, weights_imag, aligned, phases, out):
+    width = phases.shape[1]
+    held, peers = out.shape[0] // 2, out.shape[1]
+    total = held * peers
+    chunk = 2 * LANES
+    for low in range(0, width, chunk):
+        high = min(low + chunk, width)
+        images = aligned[:, low:high]
+        real = jnp.dot(weights_real, images, preferred_element_type=f32)
+        imag = jnp.dot(weights_imag, images, preferred_element_type=f32)
+        u = [real[t * total : (t + 1) * total] for t in range(SHIFTS)]
+        v = [imag[t * total : (t + 1) * total] for t in range(SHIFTS)]
+        first, second = u[0], v[0]
+        for axis in range(2):
+            cosine = phases[2 * axis : 2 * axis + 1, low:high]
+            sine = phases[2 * axis + 1 : 2 * axis + 2, low:high]
+            one, two = 1 + 2 * axis, 2 + 2 * axis
+            first = first + (u[one] + u[two]) * cosine + (v[one] - v[two]) * sine
+            second = second + (v[one] + v[two]) * cosine - (u[one] - u[two]) * sine
+        for k in range(held):
+            mine = slice(k * peers, (k + 1) * peers)
+            out[k, :, low:high] = first[mine].astype(out.dtype)
+            out[held + k, :, low:high] = second[mine].astype(out.dtype)
+
+
+def weigh_kernel(rows, route_count, columns, held, cores, scores, aligned, phases, *outs_and_scratch):
+    core = lax.axis_index("core")
+    *outs, own_real, own_imag, evidence, tall, wide = outs_and_scratch
     width = phases.shape[1]
     count = aligned.shape[0]
-    cores = len(outs)
-    same_core = outs[0].shape[1]
-    owners = cores * same_core
-    held = outs[0].shape[0] // 2
-    total = held * owners
+    each = own_real.shape[0]
+    peers = each // (SHIFTS * held)
     height = scores.shape[1]
     blocks = count // (2 * height)
     listings = scores.shape[2] // blocks
@@ -311,10 +325,10 @@
     evidence[...] = jnp.broadcast_to(log_evidence, evidence.shape)
     listed_weights = jnp.exp(values - log_evidence).astype(bf16)
     notes = aligned[:, width : width + LANES].astype(f32)
-    direction, spot = lane_facts(total, owners, same_core, columns, place[1])
+    direction, spot = block_facts(held, peers, cores, columns, core)
     spots = listings // route_count
     spread = spot_table(spot, spots)
-    weights = jnp.zeros((count, SHIFTS * total), f32)
+    weights = jnp.zeros((count, each * cores), f32)
     for r in range(route_count):
         placed = jnp.dot(
             listed_weights[:, r * spots : (r + 1) * spots], spread, preferred_element_type=f32
@@ -327,27 +341,15 @@
         first_half = first_half | ((row >= at) & (row < at + rows))
     weights_real = jnp.where(first_half, weights, 0.0).T.astype(bf16)
     weights_imag = jnp.where(first_half, 0.0, weights).T.astype(bf16)
-    chunk = 2 * LANES
-    for low in range(0, width, chunk):
-        high = min(low + chunk, width)
-        images = aligned[:, low:high]
-        real = jnp.dot(weights_real, images, preferred_element_type=f32)
-        imag = jnp.dot(weights_imag, images, preferred_element_type=f32)
-        u = [real[t * total : (t + 1) * total] for t in range(SHIFTS)]
-        v = [imag[t * total : (t + 1) * total] for t in range(SHIFTS)]
-        first, second = u[0], v[0]
-        for axis in range(2):
-            cosine = phases[2 * axis : 2 * axis + 1, low:high]
-            sine = phases[2 * axis + 1 : 2 * axis + 2, low:high]
-            one, two = 1 + 2 * axis, 2 + 2 * axis
-            first = first + (u[one] + u[two]) * cosine + (v[one] - v[two]) * sine
-            second = second + (v[one] + v[two]) * cosine - (u[one] - u[two]) * sine
-        for k in range(held):
-            for step, out in enumerate(outs):
-                start = k * owners + step * same_core
-                mine = slice(start, start + same_core)
-                out[k, :, low:high] = first[mine].astype(out.dtype)
-                out[held + k, :, low:high] = second[mine].astype(out.dtype)
+    own_real[...] = weights_real[0:each]
+    own_imag[...] = weights_imag[0:each]
+    for step, out in enumerate(outs, 1):
+        block = slice(step * each, (step + 1) * each)
+        turn_back(weights_real[block], weights_imag[block], aligned, phases, out)
+
+
+def own_kernel(weights_real, weights_imag, aligned, phases, out):
+    turn_back(weights_real[...], weights_imag[...], aligned, phases, out)
 
 
 def expectation(particles, projections, ctf, defocus_group, offsets, routes):
@@ -370,9 +372,6 @@
     params = pltpu.CompilerParams(vmem_limit_bytes=min(60 << 20, (8 << 20) + total * (88 << 10)))
 
     steps = [0] + sorted(range(1, pieces), key=exchange_order)
-    where = jnp.stack([place, lax.axis_index("core")])
-    scalars = pl.BlockSpec(memory_space=pltpu.SMEM)
-    vectors = pl.BlockSpec(memory_space=pltpu.VMEM)
     distant = (
         projections.reshape(held, 2 * pixel_count),
         particles,
@@ -439,7 +438,6 @@
             jax.ShapeDtypeStruct((pieces, count // folds, folds * listings), f32),
             jax.ShapeDtypeStruct((pieces, 2 * rows, width + LANES), bf16),
         ),
-        in_specs=[vectors] * (pieces + 2 * cores) + [scalars],
         scratch_shapes=[
             pltpu.VMEM((count, SHIFTS * total), f32),
             pltpu.VMEM((count, LANES), f32),
@@ -447,28 +445,41 @@
         ],
         compiler_params=params,
         name="score",
-    )(*parts, *turned, *energies, where)
+    )(*parts, *turned, *energies)
     aligned = aligned.reshape(pieces * 2 * rows, width + LANES)
 
     scores = lax.all_to_all(scores, group, split_axis=0, concat_axis=0, tiled=True)
 
-    kinds = [f32] + [bf16] * (cores - 1)
-    *sums, evidence = pl.pallas_call(
-        functools.partial(sums_kernel, rows, route_count, columns),
+    each = SHIFTS * held * peers
+    block = (2 * held, peers, width)
+    *sums, own_real, own_imag, evidence = pl.pallas_call(
+        functools.partial(weigh_kernel, rows, route_count, columns, held, cores),
         out_shape=(
-            *(jax.ShapeDtypeStruct((2 * held, peers, width), kind) for kind in kinds),
-            jax.ShapeDtypeStruct((2 * pieces * rows, LANES), f32),
+            *[jax.ShapeDtypeStruct(block, bf16)] * (cores - 1),
+            *[jax.ShapeDtypeStruct((each, 2 * count), bf16)] * 2,
+            jax.ShapeDtypeStruct((2 * count, LANES), f32),
         ),
-        in_specs=[vectors] * 3 + [scalars],
         scratch_shapes=[pltpu.VMEM((count, listings), f32), pltpu.VMEM((2 * count, listings), f32)],
         compiler_params=params,
-        name="sums",
-    )(scores, aligned, phases, where)
+        name="weigh",
+    )(scores, aligned, phases)
+    sums = [
+        lax.ppermute(array, "core", routes_of(step, cores))
+        for step, array in enumerate(sums, 1)
+    ]
+    merged = pl.pallas_call(
+        own_kernel,
+        out_shape=jax.ShapeDtypeStruct(block, f32),
+        compiler_params=params,
+        cost_estimate=pl.CostEstimate(
+            flops=8 * each * count * width, bytes_accessed=4 << 20, transcendentals=0
+        ),
+        name="own",
+    )(own_real, own_imag, aligned, phases)
     log_evidence = lax.dynamic_slice_in_dim(evidence, place * 2 * rows, rows, 0)[:, 0]
 
-    merged = sums[0]
-    for step in range(1, cores):
-        merged = merged + lax.ppermute(sums[step], "core", routes_of(step, cores)).astype(f32)
+    for array in sums:
+        merged = merged + array.astype(f32)
     merged = merged.astype(bf16).transpose(1, 0, 2)
     merged = lax.all_to_all(merged, same_core, split_axis=0, concat_axis=0, tiled=True)
     data_sum = jnp.sum(merged.reshape(far, pieces, 2 * held, width).astype(f32), axis=0)

time: 67.9 us -> 66.8 us (0.984)
  Pallas kernels: 9.29 us -> 8.39 us
    pallas_call x1 -> x2, Pallas kernels: 2.17 us -> 1.82 us  [the longest x1 1.26 us: expectation(): pl.pallas_call(functools.partial(weigh_kernel, rows, route_count, columns...]
  transfers between devices with their start and end apart: 11 -> 11, of which waited for: 6 -> 6; matrix products, arithmetic and copies ran while one was open for 2% -> 2% of each run, Pallas kernels for 2% -> 3%
where the time goes in v3:
time: 66.8 us; the launch traced here: 66.5 us
  starting transfers between devices  21.6 us (32%)
  waiting for transfers between devices  21.3 us (32%)
  blocking collectives  11.2 us (17%)
  Pallas kernels  8.39 us (13%)
  local copies, waits for them, and re-layouts  2.37 us (4%)
  other arithmetic  0.9 us (1%)
  between operations  0.82 us (1%)
    all_to_all x1, blocking collectives, expectation(): lax.all_to_all(scores, group, split_axis=0, concat_axis=0, tiled=True)  11.2 us
    all_to_all x1, waiting for transfers between devices, expectation(): lax.all_to_all(merged, same_core, split_axis=0, concat_axis=0, tiled=True)  10.3 us
    ppermute x7, starting transfers between devices, expectation(): parts[at] = lax.ppermute(parts[at], group, routes_of(steps[at], pieces))  9.41 us
    all_to_all x1, starting transfers between devices, expectation(): lax.all_to_all(refs, same_core, split_axis=0, concat_axis=0, tiled=True)  8.49 us
    all_to_all x1, waiting for transfers between devices, expectation(): lax.all_to_all(refs, same_core, split_axis=0, concat_axis=0, tiled=True)  5.69 us
    ppermute x7, waiting for transfers between devices, expectation(): parts[at] = lax.ppermute(parts[at], group, routes_of(steps[at], pieces))  4.32 us
    pallas_call x1, Pallas kernels, expectation(): pl.pallas_call(functools.partial(prepare_kernel, pixel_count, width, step...  3.58 us
    all_to_all x1, starting transfers between devices, expectation(): lax.all_to_all(merged, same_core, split_axis=0, concat_axis=0, tiled=True)  3.53 us
  transfers between devices with their start and end apart: 11, of which 6 were waited for; matrix products, arithmetic and copies ran while one was open for 2% of the time, Pallas kernels for 3%

profile of v3, /device:TPU:0, one launch (start us, length us, event | category | flops | bytes accessed | tf_op | source)
XLA Modules:
  0.0 66.5 jit_solution(14953830097467286190)
XLA Ops:
  0.6 3.6 %prepare.1 = (bf16[16,4,2176]{2,1,0:T(4,128)(2,1)}, bf16[24,2304]{1,0:T(8,128)(2,1)}, bf16[24,2304]{1,0:T(8,128)(2,1)}, bf16[24,2304]{1,0:T(8,128)(2,1)}, bf16[2...) custom-call(bf16[2,33024]{1,0:T(2,128)(2,1)} %bitcast.29, ...), custom_call_target="tpu_custom_call" | custom-call | tf_op jit(solution)/shard_map/prepare/pallas_call | solution.py:386
  4.3 0.0 copy-start
  4.3 8.5 %all-to-all-start = ((bf16[16,4,2176]{2,1,0:T(4,128)(2,1)}), bf16[16,4,2176]{2,1,0:T(4,128)(2,1)S(1)}, u32[]{:S(2)}, u32[]{:S(2)}) async-start(bf16[16,4,2176]{2,1,0:T(4,128)(2,1)} %get-tuple-element.29), calls=%async_computation | async-start | bytes 557056 | tf_op jit(solution)/shard_map/all_to_all | solution.py:403
  12.8 3.7 %collective-permute-start = (bf16[24,2304]{1,0:T(8,128)(2,1)}, bf16[24,2304]{1,0:T(8,128)(2,1)S(1)}, u32[]{:S(2)}, u32[]{:S(2)}) collective-permute-start(bf16[24,2304]{1,0:T(8,128)(2,1)} %get-tuple-element.22), channel_id=1, source_target_pairs={{0,11},{1,10},{2,9},{3,8},{8,3},{9,2},{10,1},{11,0},{4,15},{5,14},... | collective-permute-start | bytes 331784 | tf_op jit(solution)/shard_map/ppermute | solution.py:408
  16.5 0.6 collective-permute-start.1
  17.1 0.6 collective-permute-start.2
  17.6 0.2 collective-permute-start.3
  17.8 0.1 fusion.3
  17.9 5.7 %all-to-all-done = bf16[16,4,2176]{2,1,0:T(4,128)(2,1)S(1)} async-done(((bf16[16,4,2176]{2,1,0:T(4,128)(2,1)}), bf16[16,4,2176]{2,1,0:T(4,128)(2,1)S(1)}, u32[]{:S(2)}, u32[]{:S(2)}) %all-to-all-start) | async-done | bytes 278560 | tf_op jit(solution)/shard_map/all_to_all | solution.py:403
  23.6 0.1 collective-permute-start.7
  23.7 0.5 fusion.7
  24.2 0.5 collective-permute-done.refs_all_1_
  24.7 0.2 collective-permute-start.4
  24.9 1.9 %collective-permute-start.5 = (bf16[24,2304]{1,0:T(8,128)(2,1)S(1)}, bf16[24,2304]{1,0:T(8,128)(2,1)S(1)}, u32[]{:S(2)}, u32[]{:S(2)}) collective-permute-start(bf16[24,2304]{1,0:T(8,128)(2,1)S(1)} %copy-done.3), channel_id=1, source_target_pairs={{0,9},{1,8},{2,11},{3,10},{8,1},{9,0},{10,3},{11,2},{4,13},{5,12},... | collective-permute-start | bytes 331784 | tf_op jit(solution)/shard_map/ppermute | solution.py:408
  26.9 0.0 collective-permute-done.7
  26.9 2.2 %collective-permute-start.6 = (bf16[24,2304]{1,0:T(8,128)(2,1)S(1)}, bf16[24,2304]{1,0:T(8,128)(2,1)S(1)}, u32[]{:S(2)}, u32[]{:S(2)}) collective-permute-start(bf16[24,2304]{1,0:T(8,128)(2,1)S(1)} %copy-done.2), channel_id=1, source_target_pairs={{0,10},{1,11},{2,8},{3,9},{8,2},{9,3},{10,0},{11,1},{4,14},{5,15},... | collective-permute-start | bytes 331784 | tf_op jit(solution)/shard_map/ppermute | solution.py:408
  29.2 0.6 shard_map.77
  29.8 0.6 shard_map.78
  30.4 2.1 %collective-permute-done.4.refs_all_5_ = bf16[24,2304]{1,0:T(8,128)(2,1)S(1)} collective-permute-done((bf16[24,2304]{1,0:T(8,128)(2,1)S(1)}, bf16[24,2304]{1,0:T(8,128)(2,1)S(1)}, u32[]{:S(2)}, u32[]{:S(2)}) %collective-permute-start.4) | collective-permute-done | bytes 110624 | tf_op jit(solution)/shard_map/ppermute | solution.py:408
  32.5 1.8 %collective-permute-done.6.refs_all_7_ = bf16[24,2304]{1,0:T(8,128)(2,1)S(1)} collective-permute-done((bf16[24,2304]{1,0:T(8,128)(2,1)S(1)}, bf16[24,2304]{1,0:T(8,128)(2,1)S(1)}, u32[]{:S(2)}, u32[]{:S(2)}) %collective-permute-start.6) | collective-permute-done | bytes 110624 | tf_op jit(solution)/shard_map/ppermute | solution.py:408
  34.3 1.8 %score.1 = (f32[8,24,640]{2,1,0:T(8,128)S(1)}, bf16[8,24,2304]{2,1,0:T(8,128)(2,1)S(1)}) custom-call(bf16[24,2304]{1,0:T(8,128)(2,1)S(1)} %copy-done, bf16[24,2304]{1,0:T(8,128)(2,1)S(1)} %collective-permute-done.refs_all_1_, bf16[24,2304]{1,0:T(8,128)(2,1)S(1)} %collective-permute-done.1.refs_all_2_, ...), custom_call_target="tpu_custom_call" | custom-call | tf_op jit(solution)/shard_map/score/pallas_call | solution.py:435
  36.1 11.2 %all_to_all.15.scores = f32[8,24,640]{2,1,0:T(8,128)S(1)} all-to-all(f32[8,24,640]{2,1,0:T(8,128)S(1)} %get-tuple-element.34), channel_id=1, replica_groups=mesh['groups'=1,'far'=2,'near'=2,'core'=2,'cls'=4] {'near','cls'}, dimensions={0} | all-to-all | bytes 983040 | tf_op jit(solution)/shard_map/all_to_all | solution.py:451
  47.2 1.3 %weigh.1 = (bf16[4,16,2176]{2,1,0:T(8,128)(2,1)S(1)}, bf16[160,192]{1,0:T(8,128)(2,1)S(1)}, bf16[160,192]{1,0:T(8,128)(2,1)S(1)}, f32[192,128]{1,0:T(8,128)S(1)}) custom-call(f32[8,24,640]{2,1,0:T(8,128)S(1)} %all_to_all.15.scores, bf16[192,2304]{1,0:T(8,128)(2,1)S(1)} %bitcast.23, f32[4,2176]{1,0:T(4,128)S(1)} %reshape.113.phases), custom_call_target="tpu_custom_call" | custom-call | tf_op jit(solution)/shard_map/weigh/pallas_call | solution.py:455
  48.5 0.1 collective-permute-start.8
  48.6 0.6 own.1
  49.1 1.0 %collective-permute-done.8 = bf16[4,16,2176]{2,1,0:T(8,128)(2,1)S(1)} collective-permute-done((bf16[4,16,2176]{2,1,0:T(8,128)(2,1)S(1)}, bf16[4,16,2176]{2,1,0:T(8,128)(2,1)S(1)}, u32[]{:S(2)}, u32[]{:S(2)}) %collective-permute-start.8) | collective-permute-done | bytes 278560 | tf_op jit(solution)/shard_map/ppermute | solution.py:467
  50.2 0.8 %copy.17 = bf16[16,4,2176]{2,1,0:T(4,128)(2,1)} copy(bf16[16,4,2176]{2,0,1:T(8,128)(2,1)S(1)} %fusion) | data formatting | bytes 557056 | tf_op jit(solution)/shard_map/transpose | solution.py:483
  51.0 3.5 %all-to-all-start.2 = ((bf16[16,4,2176]{2,1,0:T(4,128)(2,1)}), bf16[16,4,2176]{2,1,0:T(4,128)(2,1)S(1)}, u32[]{:S(2)}, u32[]{:S(2)}) async-start(bf16[16,4,2176]{2,1,0:T(4,128)(2,1)} %copy.17), calls=%async_computation.2 | async-start | bytes 557056 | tf_op jit(solution)/shard_map/all_to_all | solution.py:484
  54.5 0.6 dynamic-slice_reduce_fusion
  55.2 10.3 %all-to-all-done.2 = bf16[16,4,2176]{2,1,0:T(4,128)(2,1)S(1)} async-done(((bf16[16,4,2176]{2,1,0:T(4,128)(2,1)}), bf16[16,4,2176]{2,1,0:T(4,128)(2,1)S(1)}, u32[]{:S(2)}, u32[]{:S(2)}) %all-to-all-start.2) | async-done | bytes 278560 | tf_op jit(solution)/shard_map/all_to_all | solution.py:484
  65.4 0.2 reduce_sum.12
  65.7 0.7 %slice.8 = bf16[2,2,16512]{2,0,1:T(2,128)(2,1)} slice(bf16[2,2,17408]{2,0,1:T(2,128)(2,1)S(1)} %reshape.117), slice={[0:2], [0:2], [0:16512]} | slice | bytes 264192 | tf_op jit(solution)/shard_map/slice | solution.py:487
  (20 shorter events, 0.3 us)
Async XLA Ops:
  0.6 17.2 %copy-start.1 = (bf16[8,16512]{1,0:T(8,128)(2,1)S(1)}, bf16[8,16512]{1,0:T(8,128)(2,1)}, u32[]{:S(2)}) copy-start(bf16[8,16512]{1,0:T(8,128)(2,1)} %refs_2_.1) | copy-start | bytes 792580
  4.2 20.5 %copy-start.4 = (bf16[24,2304]{1,0:T(8,128)(2,1)S(1)}, bf16[24,2304]{1,0:T(8,128)(2,1)}, u32[]{:S(2)}) copy-start(bf16[24,2304]{1,0:T(8,128)(2,1)} %get-tuple-element.26) | copy-start | bytes 331780
  4.2 20.7 %copy-start.3 = (bf16[24,2304]{1,0:T(8,128)(2,1)S(1)}, bf16[24,2304]{1,0:T(8,128)(2,1)}, u32[]{:S(2)}) copy-start(bf16[24,2304]{1,0:T(8,128)(2,1)} %get-tuple-element.27) | copy-start | bytes 331780
  4.2 22.6 %copy-start.2 = (bf16[24,2304]{1,0:T(8,128)(2,1)S(1)}, bf16[24,2304]{1,0:T(8,128)(2,1)}, u32[]{:S(2)}) copy-start(bf16[24,2304]{1,0:T(8,128)(2,1)} %get-tuple-element.28) | copy-start | bytes 331780
  4.3 30.0 %copy-start = (bf16[24,2304]{1,0:T(8,128)(2,1)S(1)}, bf16[24,2304]{1,0:T(8,128)(2,1)}, u32[]{:S(2)}) copy-start(bf16[24,2304]{1,0:T(8,128)(2,1)} %get-tuple-element.21.refs_all_0_) | copy-start | bytes 331780
  4.3 19.3 %all-to-all-start = ((bf16[16,4,2176]{2,1,0:T(4,128)(2,1)}), bf16[16,4,2176]{2,1,0:T(4,128)(2,1)S(1)}, u32[]{:S(2)}, u32[]{:S(2)}) async-start(bf16[16,4,2176]{2,1,0:T(4,128)(2,1)} %get-tuple-element.29), calls=%async_computation | async-start | bytes 557056 | tf_op jit(solution)/shard_map/all_to_all | solution.py:403
  12.8 11.9 %collective-permute-start = (bf16[24,2304]{1,0:T(8,128)(2,1)}, bf16[24,2304]{1,0:T(8,128)(2,1)S(1)}, u32[]{:S(2)}, u32[]{:S(2)}) collective-permute-start(bf16[24,2304]{1,0:T(8,128)(2,1)} %get-tuple-element.22), channel_id=1, source_target_pairs={{0,11},{1,10},{2,9},{3,8},{8,3},{9,2},{10,1},{11,0},{4,15},{5,14},... | collective-permute-start | bytes 331784 | tf_op jit(solution)/shard_map/ppermute | solution.py:408
  16.5 8.5 %collective-permute-start.1 = (bf16[24,2304]{1,0:T(8,128)(2,1)}, bf16[24,2304]{1,0:T(8,128)(2,1)S(1)}, u32[]{:S(2)}, u32[]{:S(2)}) collective-permute-start(bf16[24,2304]{1,0:T(8,128)(2,1)} %get-tuple-element.23), channel_id=1, source_target_pairs={{0,1},{1,0},{2,3},{3,2},{8,9},{9,8},{10,11},{11,10},{4,5},{5,4},{6... | collective-permute-start | bytes 331784 | tf_op jit(solution)/shard_map/ppermute | solution.py:408
  17.1 13.4 %collective-permute-start.2 = (bf16[24,2304]{1,0:T(8,128)(2,1)}, bf16[24,2304]{1,0:T(8,128)(2,1)S(1)}, u32[]{:S(2)}, u32[]{:S(2)}) collective-permute-start(bf16[24,2304]{1,0:T(8,128)(2,1)} %get-tuple-element.24), channel_id=1, source_target_pairs={{0,2},{1,3},{2,0},{3,1},{8,10},{9,11},{10,8},{11,9},{4,6},{5,7},{6... | collective-permute-start | bytes 331784 | tf_op jit(solution)/shard_map/ppermute | solution.py:408
  17.6 12.8 %collective-permute-start.3 = (bf16[24,2304]{1,0:T(8,128)(2,1)}, bf16[24,2304]{1,0:T(8,128)(2,1)S(1)}, u32[]{:S(2)}, u32[]{:S(2)}) collective-permute-start(bf16[24,2304]{1,0:T(8,128)(2,1)} %get-tuple-element.25), channel_id=1, source_target_pairs={{0,8},{1,9},{2,10},{3,11},{8,0},{9,1},{10,2},{11,3},{4,12},{5,13},... | collective-permute-start | bytes 331784 | tf_op jit(solution)/shard_map/ppermute | solution.py:408
  23.6 3.2 %collective-permute-start.7 = (bf16[16,4,2176]{2,0,1:T(8,128)(2,1)S(1)}, bf16[16,4,2176]{2,0,1:T(8,128)(2,1)S(1)}, u32[]{:S(2)}, u32[]{:S(2)}) collective-permute-start(bf16[16,4,2176]{2,0,1:T(8,128)(2,1)S(1)} %copy.22), channel_id=1, source_target_pairs={{0,4},{4,0},{1,5},{5,1},{2,6},{6,2},{3,7},{7,3},{8,12},{12,8},{9,1... | collective-permute-start | bytes 835592 | tf_op jit(solution)/shard_map/ppermute | solution.py:404
  24.7 7.8 %collective-permute-start.4 = (bf16[24,2304]{1,0:T(8,128)(2,1)S(1)}, bf16[24,2304]{1,0:T(8,128)(2,1)S(1)}, u32[]{:S(2)}, u32[]{:S(2)}) collective-permute-start(bf16[24,2304]{1,0:T(8,128)(2,1)S(1)} %copy-done.4), channel_id=1, source_target_pairs={{0,3},{1,2},{2,1},{3,0},{8,11},{9,10},{10,9},{11,8},{4,7},{5,6},{6... | collective-permute-start | bytes 331784 | tf_op jit(solution)/shard_map/ppermute | solution.py:408
  24.9 7.6 %collective-permute-start.5 = (bf16[24,2304]{1,0:T(8,128)(2,1)S(1)}, bf16[24,2304]{1,0:T(8,128)(2,1)S(1)}, u32[]{:S(2)}, u32[]{:S(2)}) collective-permute-start(bf16[24,2304]{1,0:T(8,128)(2,1)S(1)} %copy-done.3), channel_id=1, source_target_pairs={{0,9},{1,8},{2,11},{3,10},{8,1},{9,0},{10,3},{11,2},{4,13},{5,12},... | collective-permute-start | bytes 331784 | tf_op jit(solution)/shard_map/ppermute | solution.py:408
  26.9 7.4 %collective-permute-start.6 = (bf16[24,2304]{1,0:T(8,128)(2,1)S(1)}, bf16[24,2304]{1,0:T(8,128)(2,1)S(1)}, u32[]{:S(2)}, u32[]{:S(2)}) collective-permute-start(bf16[24,2304]{1,0:T(8,128)(2,1)S(1)} %copy-done.2), channel_id=1, source_target_pairs={{0,10},{1,11},{2,8},{3,9},{8,2},{9,3},{10,0},{11,1},{4,14},{5,15},... | collective-permute-start | bytes 331784 | tf_op jit(solution)/shard_map/ppermute | solution.py:408
  48.5 1.6 %collective-permute-start.8 = (bf16[4,16,2176]{2,1,0:T(8,128)(2,1)S(1)}, bf16[4,16,2176]{2,1,0:T(8,128)(2,1)S(1)}, u32[]{:S(2)}, u32[]{:S(2)}) collective-permute-start(bf16[4,16,2176]{2,1,0:T(8,128)(2,1)S(1)} %get-tuple-element.39), channel_id=1, source_target_pairs={{0,4},{4,0},{1,5},{5,1},{2,6},{6,2},{3,7},{7,3},{8,12},{12,8},{9,1... | collective-permute-start | bytes 835592 | tf_op jit(solution)/shard_map/ppermute | solution.py:467
  51.0 14.4 %all-to-all-start.2 = ((bf16[16,4,2176]{2,1,0:T(4,128)(2,1)}), bf16[16,4,2176]{2,1,0:T(4,128)(2,1)S(1)}, u32[]{:S(2)}, u32[]{:S(2)}) async-start(bf16[16,4,2176]{2,1,0:T(4,128)(2,1)} %copy.17), calls=%async_computation.2 | async-start | bytes 557056 | tf_op jit(solution)/shard_map/all_to_all | solution.py:484

commit v4 on v3

--- a/solution.py
+++ b/solution.py
@@ -63,25 +63,46 @@
     return [(i, int(other(i, step, size))) for i in range(size)]
 
 
-def split_refs(pixel_count, width, refs, out):
-    held = refs.shape[0]
-    pieces = -(-pixel_count // width)
+def layout(pixel_count, pieces, facts):
+    main = pixel_count // (pieces * LANES) * LANES
+    share = -(-(pixel_count - pieces * main) // pieces)
+    width = main + LANES * (1 if share + facts <= LANES else 2)
+    return main, share, width, share if width == main + LANES else 0
+
+
+def split_refs(pixel_count, main, share, refs, out):
+    held, width = refs.shape[0], out.shape[2]
+    pieces = pixel_count // main if share == 0 else (pixel_count - 1) // (main + share) + 1
+    for half in range(2):
+        start = half * pixel_count
+        left = refs[:, start + pieces * main : start + pixel_count].astype(f32)
+        for piece in range(pieces):
+            tail = left[:, piece * share : (piece + 1) * share]
+            empty = jnp.zeros((held, width - main - tail.shape[1]), f32)
+            tail = jnp.concatenate([tail, empty], axis=1).astype(bf16)
+            values = refs[:, start + piece * main : start + (piece + 1) * main]
+            for copy in range(piece, out.shape[0], pieces):
+                out[copy, half * held : (half + 1) * held, 0:main] = values
+                out[copy, half * held : (half + 1) * held, main:width] = tail
+
+
+def own_ctf(pixel_count, plan, pieces, place, ctf, out):
+    main, share, width, _ = plan
+    for low in range(0, main, LANES):
+        start = pl.multiple_of(place * main + low, LANES)
+        out[:, low : low + LANES] = ctf[:, pl.ds(start, LANES)]
+    left = ctf[:, pieces * main : pixel_count].astype(f32)
+    tail = jnp.zeros((ctf.shape[0], width - main), f32)
     for piece in range(pieces):
-        low = piece * width
-        size = min(width, pixel_count - low)
-        for half in range(2):
-            values = refs[:, half * pixel_count + low : half * pixel_count + low + size]
-            for copy in range(piece, out.shape[0], pieces):
-                out[copy, half * held : (half + 1) * held, 0:size] = values
-                if size < width:
-                    out[copy, half * held : (half + 1) * held, size:width] = jnp.zeros(
-                        (held, width - size), bf16
-                    )
-
-
-def prepare_kernel(pixel_count, width, steps, group, *refs):
-    distant, (split, *outs), rest = refs[:6], refs[6 : 7 + len(steps)], refs[7 + len(steps) :]
-    near, (split_here, whole, ctf_rows, table, arrived, left) = rest[:6], rest[6:]
+        mine = left[:, piece * share : (piece + 1) * share]
+        empty = jnp.zeros((ctf.shape[0], width - main - mine.shape[1]), f32)
+        tail = jnp.where(place == piece, jnp.concatenate([mine, empty], axis=1), tail)
+    out[:, main:width] = tail.astype(bf16)
+
+
+def prepare_kernel(pixel_count, plan, steps, group, *refs):
+    distant, (split, ctf_out, *outs), rest = refs[:6], refs[6 : 8 + len(steps)], refs[8 + len(steps) :]
+    near, (split_here, ctf_here, whole, ctf_rows, table, arrived, left) = rest[:6], rest[6:]
     copies = [
         pltpu.make_async_copy(far, here, arrived.at[i])
         for i, (far, here) in enumerate(zip(distant, near))
@@ -89,13 +110,16 @@
     for copy in copies:
         copy.start()
     copies[0].wait()
-    split_refs(pixel_count, width, near[0], split_here)
+    split_refs(pixel_count, *plan[:2], near[0], split_here)
     sent = [pltpu.make_async_copy(split_here, split, left.at[0])]
     sent[0].start()
     for copy in copies[2:]:
         copy.wait()
-    align(pixel_count, width, *near[1:], whole, ctf_rows, table, copies[1])
     place = lax.axis_index(group)
+    own_ctf(pixel_count, plan, len(steps), place, near[2], ctf_here)
+    sent.append(pltpu.make_async_copy(ctf_here, ctf_out, left.at[1]))
+    sent[1].start()
+    align(pixel_count, plan, *near[1:], whole, ctf_rows, table, copies[1])
     for step, out in zip(steps, outs):
         piece = whole.at[other(place, step, len(steps))]
         sent.append(pltpu.make_async_copy(piece, out, left.at[len(sent)]))
@@ -105,7 +129,7 @@
 
 
 def align(
-    pixel_count, width, images, ctf, groups, offsets, routes, whole, ctf_rows, table, coming
+    pixel_count, plan, images, ctf, groups, offsets, routes, whole, ctf_rows, table, coming
 ):
     rows = images.shape[0]
     pieces = whole.shape[0]
@@ -134,33 +158,41 @@
     start = lax.broadcasted_iota(jnp.int32, (rows, blocks), 1) * (block // KY)
     start_cos, start_sin = unit_circle(start.astype(f32) * shift_across)
     coming.wait()
+
+    def tile(low):
+        turn, step = divmod(low // LANES, per_block)
+        bc = base_cos[:, step * LANES : (step + 1) * LANES]
+        bs = base_sin[:, step * LANES : (step + 1) * LANES]
+        rc = start_cos[:, turn : turn + 1]
+        rs = start_sin[:, turn : turn + 1]
+        cosine = bc * rc - bs * rs
+        sine = bs * rc + bc * rs
+        scale = ctf_rows[:, low : low + LANES]
+        real = images[:, low : low + LANES].astype(f32)
+        imag = images[:, pixel_count + low : pixel_count + low + LANES].astype(f32)
+        first = (real * cosine + imag * sine) * scale
+        second = (imag * cosine - real * sine) * scale
+        return jnp.concatenate([first, second], axis=0)
+
+    main, share, width, spare = plan
     for piece in range(pieces):
-        for part in range(width // LANES):
-            low = piece * width + part * LANES
-            here = slice(part * LANES, (part + 1) * LANES)
-            if low >= pixel_count:
-                whole[piece, :, here] = jnp.zeros((2 * rows, LANES), bf16)
-                continue
-            turn, step = divmod(low // LANES, per_block)
-            bc = base_cos[:, step * LANES : (step + 1) * LANES]
-            bs = base_sin[:, step * LANES : (step + 1) * LANES]
-            rc = start_cos[:, turn : turn + 1]
-            rs = start_sin[:, turn : turn + 1]
-            cosine = bc * rc - bs * rs
-            sine = bs * rc + bc * rs
-            scale = ctf_rows[:, low : low + LANES]
-            real = images[:, low : low + LANES].astype(f32)
-            imag = images[:, pixel_count + low : pixel_count + low + LANES].astype(f32)
-            first = (real * cosine + imag * sine) * scale
-            second = (imag * cosine - real * sine) * scale
-            whole[piece, :, here] = jnp.concatenate([first, second], axis=0).astype(bf16)
+        for low in range(0, main, LANES):
+            whole[piece, :, low : low + LANES] = tile(piece * main + low).astype(bf16)
+    left = [tile(low) for low in range(pieces * main, pixel_count, LANES)]
     lane = lax.broadcasted_iota(jnp.int32, (rows, LANES), 1)
-    notes = jnp.where(lane == route_count, group, 0.0)
+    notes = jnp.where(lane == spare + route_count, group, 0.0)
     for r in range(route_count):
-        notes = jnp.where(lane == r, facts[:, 3 + r : 4 + r], notes)
-    notes = jnp.concatenate([notes, notes], axis=0).astype(bf16)
+        notes = jnp.where(lane == spare + r, facts[:, 3 + r : 4 + r], notes)
+    notes = jnp.concatenate([notes, notes], axis=0)
+    left = jnp.concatenate(left, axis=1) if left else notes[:, 0:0]
     for piece in range(pieces):
-        whole[piece, :, width : width + LANES] = notes
+        mine = left[:, piece * share : (piece + 1) * share]
+        if width > main + LANES:
+            empty = jnp.zeros((2 * rows, width - LANES - main - mine.shape[1]), f32)
+            tail = jnp.concatenate([mine, empty, notes], axis=1)
+        else:
+            tail = jnp.concatenate([mine, notes[:, mine.shape[1] :]], axis=1)
+        whole[piece, :, main:width] = tail.astype(bf16)
 
 
 def spot_table(spot, spots):
@@ -211,7 +243,7 @@
     energy[...] = jnp.concatenate([half] * SHIFTS, axis=1)
 
 
-def score_kernel(rows, route_count, columns, held, cores, steps, *refs_all):
+def score_kernel(rows, route_count, columns, held, cores, steps, spare, *refs_all):
     count = len(steps)
     parts, blocks, energies = refs_all[:count], refs_all[count:][:cores], refs_all[count + cores :][:cores]
     out, aligned, dense, notes, packed = refs_all[count + 2 * cores :]
@@ -232,13 +264,13 @@
             )
     for at in range(count):
         mine = slice(at * rows, (at + 1) * rows)
-        notes[mine, :] = aligned[at, 0:rows, width : width + LANES].astype(f32)
+        notes[mine, :] = aligned[at, 0:rows, width - LANES : width].astype(f32)
     energy = jnp.concatenate([energy[...] for energy in energies], axis=1)
     facts = notes[...]
     values = dense[...]
     for g in range(energy.shape[0]):
         values = values - jnp.where(
-            facts[:, route_count : route_count + 1] == float(g), energy[g : g + 1, :], 0.0
+            facts[:, spare + route_count : spare + route_count + 1] == float(g), energy[g : g + 1, :], 0.0
         )
     first = values.astype(bf16)
     rest = values - first.astype(f32)
@@ -250,7 +282,7 @@
     particles = rows * count
     stacked = []
     for r in range(route_count):
-        listed = facts[:, r : r + 1] == direction
+        listed = facts[:, spare + r : spare + r + 1] == direction
         stacked += [jnp.where(listed, term, 0.0).astype(bf16) for term in terms]
     chosen = lax.dot_general(
         jnp.concatenate(stacked, axis=0),
@@ -296,7 +328,7 @@
             out[held + k, :, low:high] = second[mine].astype(out.dtype)
 
 
-def weigh_kernel(rows, route_count, columns, held, cores, scores, aligned, phases, *outs_and_scratch):
+def weigh_kernel(rows, route_count, columns, held, cores, spare, scores, aligned, phases, *outs_and_scratch):
     core = lax.axis_index("core")
     *outs, own_real, own_imag, evidence, tall, wide = outs_and_scratch
     width = phases.shape[1]
@@ -324,7 +356,7 @@
     log_evidence = peak + jnp.log(mass)
     evidence[...] = jnp.broadcast_to(log_evidence, evidence.shape)
     listed_weights = jnp.exp(values - log_evidence).astype(bf16)
-    notes = aligned[:, width : width + LANES].astype(f32)
+    notes = aligned[:, width - LANES : width].astype(f32)
     direction, spot = block_facts(held, peers, cores, columns, core)
     spots = listings // route_count
     spread = spot_table(spot, spots)
@@ -333,7 +365,7 @@
         placed = jnp.dot(
             listed_weights[:, r * spots : (r + 1) * spots], spread, preferred_element_type=f32
         )
-        weights = jnp.where(notes[:, r : r + 1] == direction, placed, weights)
+        weights = jnp.where(notes[:, spare + r : spare + r + 1] == direction, placed, weights)
     row = lax.broadcasted_iota(jnp.int32, (count, 1), 0)
     first_half = jnp.zeros((count, 1), jnp.bool_)
     for part in range(count // (2 * rows)):
@@ -352,6 +384,26 @@
     turn_back(weights_real[...], weights_imag[...], aligned, phases, out)
 
 
+def collect_kernel(far, main, share, parts, out):
+    pieces, held = parts.shape[0] // far, out.shape[0]
+    pixel_count = out.shape[1] // 2
+    tails = []
+    for piece in range(pieces):
+        total = parts[piece].astype(f32)
+        for part in range(1, far):
+            total = total + parts[part * pieces + piece].astype(f32)
+        for half in range(2):
+            low = half * pixel_count + piece * main
+            out[:, low : low + main] = total[half * held : (half + 1) * held, 0:main].astype(bf16)
+        tails.append(total[:, main : main + share])
+    left = pixel_count - pieces * main
+    if left:
+        tail = jnp.concatenate(tails, axis=1)[:, 0:left]
+        for half in range(2):
+            low = half * pixel_count + pieces * main
+            out[:, low : low + left] = tail[half * held : (half + 1) * held].astype(bf16)
+
+
 def expectation(particles, projections, ctf, defocus_group, offsets, routes):
     pixel_count = KX * KY
     rows = particles.shape[0]
@@ -365,8 +417,8 @@
     pieces = near * columns
     peers = far * pieces
     owners = peers * cores
-    width = -(-pixel_count // (pieces * LANES)) * LANES
-    padded = pieces * width
+    plan = layout(pixel_count, pieces, route_count + 1)
+    main, share, width, spare = plan
     place = lax.axis_index(group)
     total = held * owners
     params = pltpu.CompilerParams(vmem_limit_bytes=min(60 << 20, (8 << 20) + total * (88 << 10)))
@@ -381,21 +433,23 @@
         routes.T,
     )
     split = jax.ShapeDtypeStruct((peers, 2 * held, width), bf16)
-    piece = jax.ShapeDtypeStruct((2 * rows, width + LANES), bf16)
+    piece = jax.ShapeDtypeStruct((2 * rows, width), bf16)
     in_place = pl.BlockSpec(memory_space=pltpu.HBM)
-    refs, *parts = pl.pallas_call(
-        functools.partial(prepare_kernel, pixel_count, width, steps, group),
-        out_shape=[split] + [piece] * pieces,
+    own = jax.ShapeDtypeStruct((ctf.shape[0], width), bf16)
+    refs, ctf_here, *parts = pl.pallas_call(
+        functools.partial(prepare_kernel, pixel_count, plan, steps, group),
+        out_shape=[split, own] + [piece] * pieces,
         in_specs=[in_place] * len(distant),
-        out_specs=[in_place] * (1 + pieces),
+        out_specs=[in_place] * (2 + pieces),
         scratch_shapes=[pltpu.VMEM(array.shape, array.dtype) for array in distant]
         + [
             pltpu.VMEM(split.shape, bf16),
-            pltpu.VMEM((pieces, 2 * rows, width + LANES), bf16),
+            pltpu.VMEM(own.shape, bf16),
+            pltpu.VMEM((pieces, 2 * rows, width), bf16),
             pltpu.VMEM((rows, pixel_count), f32),
             pltpu.VMEM((-(-(3 + route_count) // 8) * 8, -(-rows // LANES) * LANES), f32),
             pltpu.SemaphoreType.DMA((len(distant),)),
-            pltpu.SemaphoreType.DMA((1 + pieces,)),
+            pltpu.SemaphoreType.DMA((2 + pieces,)),
         ],
         compiler_params=pltpu.CompilerParams(vmem_limit_bytes=60 << 20),
         name="prepare",
@@ -407,14 +461,11 @@
     for at in range(1, pieces):
         parts[at] = lax.ppermute(parts[at], group, routes_of(steps[at], pieces))
 
-    column = place * width + jnp.arange(width, dtype=jnp.int32)
+    lane = jnp.arange(width, dtype=jnp.int32)
+    column = lane + jnp.where(lane < main, place * main, (pieces - 1) * main + place * share)
     across, down = column // KY, column % KY - KY // 2
     angles = jnp.stack([across, down]).astype(f32) * (2.0 * math.pi / BOX)
     phases = jnp.stack([jnp.cos(angles), jnp.sin(angles)], axis=1).reshape(4, width)
-    ctf_here = lax.dynamic_slice_in_dim(
-        jnp.pad(ctf, ((0, 0), (0, padded - pixel_count))), place * width, width, 1
-    )
-
     count = pieces * rows
     listings = route_count * SHIFTS * held * columns
     folds = 4 if count % 32 == 0 else 1
@@ -433,10 +484,10 @@
         )
     )
     scores, aligned = pl.pallas_call(
-        functools.partial(score_kernel, rows, route_count, columns, held, cores, steps),
+        functools.partial(score_kernel, rows, route_count, columns, held, cores, steps, spare),
         out_shape=(
             jax.ShapeDtypeStruct((pieces, count // folds, folds * listings), f32),
-            jax.ShapeDtypeStruct((pieces, 2 * rows, width + LANES), bf16),
+            jax.ShapeDtypeStruct((pieces, 2 * rows, width), bf16),
         ),
         scratch_shapes=[
             pltpu.VMEM((count, SHIFTS * total), f32),
@@ -446,14 +497,14 @@
         compiler_params=params,
         name="score",
     )(*parts, *turned, *energies)
-    aligned = aligned.reshape(pieces * 2 * rows, width + LANES)
+    aligned = aligned.reshape(pieces * 2 * rows, width)
 
     scores = lax.all_to_all(scores, group, split_axis=0, concat_axis=0, tiled=True)
 
     each = SHIFTS * held * peers
     block = (2 * held, peers, width)
     *sums, own_real, own_imag, evidence = pl.pallas_call(
-        functools.partial(weigh_kernel, rows, route_count, columns, held, cores),
+        functools.partial(weigh_kernel, rows, route_count, columns, held, cores, spare),
         out_shape=(
             *[jax.ShapeDtypeStruct(block, bf16)] * (cores - 1),
             *[jax.ShapeDtypeStruct((each, 2 * count), bf16)] * 2,
@@ -482,9 +533,12 @@
         merged = merged + array.astype(f32)
     merged = merged.astype(bf16).transpose(1, 0, 2)
     merged = lax.all_to_all(merged, same_core, split_axis=0, concat_axis=0, tiled=True)
-    data_sum = jnp.sum(merged.reshape(far, pieces, 2 * held, width).astype(f32), axis=0)
-    data_sum = data_sum.astype(bf16).reshape(pieces, 2, held, width).transpose(2, 1, 0, 3)
-    data_sum = data_sum.reshape(held, 2, padded)[:, :, :pixel_count]
+    data_sum = pl.pallas_call(
+        functools.partial(collect_kernel, far, main, share),
+        out_shape=jax.ShapeDtypeStruct((held, 2 * pixel_count), bf16),
+        compiler_params=params,
+        name="collect",
+    )(merged)
     return (log_evidence, data_sum.reshape(projections.shape))
 
 

time: 66.8 us -> 66.7 us (level)
  local copies, waits for them, and re-layouts: 2.37 us -> 0.81 us
  Pallas kernels: 8.39 us -> 9.11 us
  other arithmetic: 0.9 us -> 1.6 us
    transpose x1, other arithmetic: 0.05 us -> 0.98 us  [expectation(): merged = merged.astype(bf16).transpose(1, 0, 2)]
    transpose x1 -> x0, local copies, waits for them, and re-layouts: 0.81 us -> none  [expectation(): merged = merged.astype(bf16).transpose(1, 0, 2)]
    slice x1 -> x0, local copies, waits for them, and re-layouts: 0.75 us -> none  [expectation(): data_sum = data_sum.reshape(held, 2, padded)[:, :, :pixel_count]]
    pallas_call x1 -> x2, Pallas kernels: 3.58 us -> 4.3 us  [the longest x1 3.56 us: expectation(): pl.pallas_call(functools.partial(prepare_kernel, pixel_count, plan, steps...]
where the time goes in v4:
time: 66.7 us; the launch traced here: 66.3 us
  starting transfers between devices  21.6 us (32%)
  waiting for transfers between devices  21.3 us (32%)
  blocking collectives  11.2 us (17%)
  Pallas kernels  9.11 us (14%)
  other arithmetic  1.6 us (2%)
  local copies, waits for them, and re-layouts  0.81 us (1%)
  between operations  0.77 us (1%)
    all_to_all x1, blocking collectives, expectation(): lax.all_to_all(scores, group, split_axis=0, concat_axis=0, tiled=True)  11.2 us
    all_to_all x1, waiting for transfers between devices, expectation(): lax.all_to_all(merged, same_core, split_axis=0, concat_axis=0, tiled=True)  10.3 us
    ppermute x7, starting transfers between devices, expectation(): parts[at] = lax.ppermute(parts[at], group, routes_of(steps[at], pieces))  9.4 us
    all_to_all x1, starting transfers between devices, expectation(): lax.all_to_all(refs, same_core, split_axis=0, concat_axis=0, tiled=True)  8.49 us
    all_to_all x1, waiting for transfers between devices, expectation(): lax.all_to_all(refs, same_core, split_axis=0, concat_axis=0, tiled=True)  5.75 us
    ppermute x7, waiting for transfers between devices, expectation(): parts[at] = lax.ppermute(parts[at], group, routes_of(steps[at], pieces))  4.26 us
    pallas_call x1, Pallas kernels, expectation(): pl.pallas_call(functools.partial(prepare_kernel, pixel_count, plan, steps...  3.56 us
    all_to_all x1, starting transfers between devices, expectation(): lax.all_to_all(merged, same_core, split_axis=0, concat_axis=0, tiled=True)  3.53 us
  transfers between devices with their start and end apart: 11, of which 6 were waited for; matrix products, arithmetic and copies ran while one was open for 2% of the time, Pallas kernels for 3%

profile of v4, /device:TPU:0, one launch (start us, length us, event | category | flops | bytes accessed | tf_op | source)
XLA Modules:
  0.0 66.3 jit_solution(5821806804473819952)
XLA Ops:
  0.6 3.6 %prepare.1 = (bf16[16,4,2176]{2,1,0:T(4,128)(2,1)}, bf16[8,2176]{1,0:T(8,128)(2,1)}, bf16[24,2176]{1,0:T(8,128)(2,1)}, bf16[24,2176]{1,0:T(8,128)(2,1)}, bf16[24...) custom-call(bf16[2,33024]{1,0:T(2,128)(2,1)} %bitcast.19, ...), custom_call_target="tpu_custom_call" | custom-call | tf_op jit(solution)/shard_map/prepare/pallas_call | solution.py:439
  4.2 0.0 copy-start.1
  4.2 8.5 %all-to-all-start = ((bf16[16,4,2176]{2,1,0:T(4,128)(2,1)}), bf16[16,4,2176]{2,1,0:T(4,128)(2,1)S(1)}, u32[]{:S(2)}, u32[]{:S(2)}) async-start(bf16[16,4,2176]{2,1,0:T(4,128)(2,1)} %get-tuple-element.30), calls=%async_computation | async-start | bytes 557056 | tf_op jit(solution)/shard_map/all_to_all | solution.py:457
  12.7 3.7 %collective-permute-start = (bf16[24,2176]{1,0:T(8,128)(2,1)}, bf16[24,2176]{1,0:T(8,128)(2,1)S(1)}, u32[]{:S(2)}, u32[]{:S(2)}) collective-permute-start(bf16[24,2176]{1,0:T(8,128)(2,1)} %get-tuple-element.23), channel_id=1, source_target_pairs={{0,11},{1,10},{2,9},{3,8},{8,3},{9,2},{10,1},{11,0},{4,15},{5,14},... | collective-permute-start | bytes 313352 | tf_op jit(solution)/shard_map/ppermute | solution.py:462
  16.4 0.6 collective-permute-start.1
  17.0 0.6 collective-permute-start.2
  17.6 0.2 collective-permute-start.3
  17.7 0.1 fusion.5
  17.8 5.8 %all-to-all-done = bf16[16,4,2176]{2,1,0:T(4,128)(2,1)S(1)} async-done(((bf16[16,4,2176]{2,1,0:T(4,128)(2,1)}), bf16[16,4,2176]{2,1,0:T(4,128)(2,1)S(1)}, u32[]{:S(2)}, u32[]{:S(2)}) %all-to-all-start) | async-done | bytes 278560 | tf_op jit(solution)/shard_map/all_to_all | solution.py:457
  23.6 0.1 collective-permute-start.7
  23.7 0.5 fusion.8
  24.2 0.3 collective-permute-done.refs_all_1_
  24.5 0.2 collective-permute-start.4
  24.8 0.0 collective-permute-done.1.refs_all_2_
  24.8 2.0 %collective-permute-start.5 = (bf16[24,2176]{1,0:T(8,128)(2,1)}, bf16[24,2176]{1,0:T(8,128)(2,1)S(1)}, u32[]{:S(2)}, u32[]{:S(2)}) collective-permute-start(bf16[24,2176]{1,0:T(8,128)(2,1)} %get-tuple-element.28), channel_id=1, source_target_pairs={{0,9},{1,8},{2,11},{3,10},{8,1},{9,0},{10,3},{11,2},{4,13},{5,12},... | collective-permute-start | bytes 313352 | tf_op jit(solution)/shard_map/ppermute | solution.py:462
  26.7 2.2 %collective-permute-start.6 = (bf16[24,2176]{1,0:T(8,128)(2,1)}, bf16[24,2176]{1,0:T(8,128)(2,1)S(1)}, u32[]{:S(2)}, u32[]{:S(2)}) collective-permute-start(bf16[24,2176]{1,0:T(8,128)(2,1)} %get-tuple-element.29), channel_id=1, source_target_pairs={{0,10},{1,11},{2,8},{3,9},{8,2},{9,3},{10,0},{11,1},{4,14},{5,15},... | collective-permute-start | bytes 313352 | tf_op jit(solution)/shard_map/ppermute | solution.py:462
  29.0 0.6 shard_map.77
  29.6 0.6 shard_map.78
  30.3 2.0 %collective-permute-done.4.refs_all_5_ = bf16[24,2176]{1,0:T(8,128)(2,1)S(1)} collective-permute-done((bf16[24,2176]{1,0:T(8,128)(2,1)}, bf16[24,2176]{1,0:T(8,128)(2,1)S(1)}, u32[]{:S(2)}, u32[]{:S(2)}) %collective-permute-start.4) | collective-permute-done | bytes 104480 | tf_op jit(solution)/shard_map/ppermute | solution.py:462
  32.3 1.9 %collective-permute-done.6.refs_all_7_ = bf16[24,2176]{1,0:T(8,128)(2,1)S(1)} collective-permute-done((bf16[24,2176]{1,0:T(8,128)(2,1)}, bf16[24,2176]{1,0:T(8,128)(2,1)S(1)}, u32[]{:S(2)}, u32[]{:S(2)}) %collective-permute-start.6) | collective-permute-done | bytes 104480 | tf_op jit(solution)/shard_map/ppermute | solution.py:462
  34.2 1.8 %score.1 = (f32[8,24,640]{2,1,0:T(8,128)S(1)}, bf16[8,24,2176]{2,1,0:T(8,128)(2,1)S(1)}) custom-call(bf16[24,2176]{1,0:T(8,128)(2,1)S(1)} %copy-done.1, bf16[24,2176]{1,0:T(8,128)(2,1)S(1)} %collective-permute-done.refs_all_1_, bf16[24,2176]{1,0:T(8,128)(2,1)S(1)} %collective-permute-done.1.refs_all_2_, ...), custom_call_target="tpu_custom_call" | custom-call | tf_op jit(solution)/shard_map/score/pallas_call | solution.py:486
  36.0 11.2 %all_to_all.15.scores = f32[8,24,640]{2,1,0:T(8,128)S(1)} all-to-all(f32[8,24,640]{2,1,0:T(8,128)S(1)} %get-tuple-element.36), channel_id=1, replica_groups=mesh['groups'=1,'far'=2,'near'=2,'core'=2,'cls'=4] {'near','cls'}, dimensions={0} | all-to-all | bytes 983040 | tf_op jit(solution)/shard_map/all_to_all | solution.py:502
  47.1 1.3 %weigh.1 = (bf16[4,16,2176]{2,1,0:T(8,128)(2,1)S(1)}, bf16[160,192]{1,0:T(8,128)(2,1)S(1)}, bf16[160,192]{1,0:T(8,128)(2,1)S(1)}, f32[192,128]{1,0:T(8,128)S(1)}) custom-call(f32[8,24,640]{2,1,0:T(8,128)S(1)} %all_to_all.15.scores, bf16[192,2176]{1,0:T(8,128)(2,1)S(1)} %bitcast.15, f32[4,2176]{1,0:T(4,128)S(1)} %reshape.113.phases), custom_call_target="tpu_custom_call" | custom-call | tf_op jit(solution)/shard_map/weigh/pallas_call | solution.py:506
  48.4 0.1 copy.16
  48.5 0.1 collective-permute-start.8
  48.6 0.6 own.1
  49.1 1.0 %collective-permute-done.8 = bf16[4,16,2176]{2,0,1:T(4,128)(2,1)S(1)} collective-permute-done((bf16[4,16,2176]{2,0,1:T(4,128)(2,1)S(1)}, bf16[4,16,2176]{2,0,1:T(4,128)(2,1)S(1)}, u32[]{:S(2)}, u32[]{:S(2)}) %collective-permute-start.8) | collective-permute-done | bytes 278560 | tf_op jit(solution)/shard_map/ppermute | solution.py:518
  50.1 1.0 %fusion.1 = bf16[16,4,2176]{2,1,0:T(4,128)(2,1)} fusion(bf16[4,16,2176]{2,0,1:T(4,128)(2,1)S(1)} %collective-permute-done.8, f32[4,16,2176]{2,1,0:T(8,128)S(1)} %own.1), kind=kLoop, calls=%fused_computation.2 | loop fusion | flops 417792 | bytes 1114112 | tf_op jit(solution)/shard_map/transpose | solution.py:534
  51.1 3.5 %all-to-all-start.2 = ((bf16[16,4,2176]{2,1,0:T(4,128)(2,1)}), bf16[16,4,2176]{2,1,0:T(4,128)(2,1)S(1)}, u32[]{:S(2)}, u32[]{:S(2)}) async-start(bf16[16,4,2176]{2,1,0:T(4,128)(2,1)} %fusion.1), calls=%async_computation.2 | async-start | bytes 557056 | tf_op jit(solution)/shard_map/all_to_all | solution.py:535
  54.7 0.6 dynamic-slice_reduce_fusion
  55.3 10.3 %all-to-all-done.2.parts = bf16[16,4,2176]{2,1,0:T(4,128)(2,1)S(1)} async-done(((bf16[16,4,2176]{2,1,0:T(4,128)(2,1)}), bf16[16,4,2176]{2,1,0:T(4,128)(2,1)S(1)}, u32[]{:S(2)}, u32[]{:S(2)}) %all-to-all-start.2) | async-done | bytes 278560 | tf_op jit(solution)/shard_map/all_to_all | solution.py:535
  65.5 0.7 %collect.1 = bf16[2,33024]{1,0:T(2,128)(2,1)} custom-call(bf16[16,4,2176]{2,1,0:T(4,128)(2,1)S(1)} %all-to-all-done.2.parts), custom_call_target="tpu_custom_call" | custom-call | tf_op jit(solution)/shard_map/collect/pallas_call | solution.py:536
  (10 shorter events, 0.1 us)
Async XLA Ops:
  4.2 24.8 %copy-start = (bf16[8,2176]{1,0:T(8,128)(2,1)S(1)}, bf16[8,2176]{1,0:T(8,128)(2,1)}, u32[]{:S(2)}) copy-start(bf16[8,2176]{1,0:T(8,128)(2,1)} %get-tuple-element.31.ctf) | copy-start | bytes 104452
  4.2 30.0 %copy-start.1 = (bf16[24,2176]{1,0:T(8,128)(2,1)S(1)}, bf16[24,2176]{1,0:T(8,128)(2,1)}, u32[]{:S(2)}) copy-start(bf16[24,2176]{1,0:T(8,128)(2,1)} %get-tuple-element.22.refs_all_0_) | copy-start | bytes 313348
  4.2 19.3 %all-to-all-start = ((bf16[16,4,2176]{2,1,0:T(4,128)(2,1)}), bf16[16,4,2176]{2,1,0:T(4,128)(2,1)S(1)}, u32[]{:S(2)}, u32[]{:S(2)}) async-start(bf16[16,4,2176]{2,1,0:T(4,128)(2,1)} %get-tuple-element.30), calls=%async_computation | async-start | bytes 557056 | tf_op jit(solution)/shard_map/all_to_all | solution.py:457
  12.7 11.8 %collective-permute-start = (bf16[24,2176]{1,0:T(8,128)(2,1)}, bf16[24,2176]{1,0:T(8,128)(2,1)S(1)}, u32[]{:S(2)}, u32[]{:S(2)}) collective-permute-start(bf16[24,2176]{1,0:T(8,128)(2,1)} %get-tuple-element.23), channel_id=1, source_target_pairs={{0,11},{1,10},{2,9},{3,8},{8,3},{9,2},{10,1},{11,0},{4,15},{5,14},... | collective-permute-start | bytes 313352 | tf_op jit(solution)/shard_map/ppermute | solution.py:462
  16.4 8.3 %collective-permute-start.1 = (bf16[24,2176]{1,0:T(8,128)(2,1)}, bf16[24,2176]{1,0:T(8,128)(2,1)S(1)}, u32[]{:S(2)}, u32[]{:S(2)}) collective-permute-start(bf16[24,2176]{1,0:T(8,128)(2,1)} %get-tuple-element.24), channel_id=1, source_target_pairs={{0,1},{1,0},{2,3},{3,2},{8,9},{9,8},{10,11},{11,10},{4,5},{5,4},{6... | collective-permute-start | bytes 313352 | tf_op jit(solution)/shard_map/ppermute | solution.py:462
  17.0 13.2 %collective-permute-start.2 = (bf16[24,2176]{1,0:T(8,128)(2,1)}, bf16[24,2176]{1,0:T(8,128)(2,1)S(1)}, u32[]{:S(2)}, u32[]{:S(2)}) collective-permute-start(bf16[24,2176]{1,0:T(8,128)(2,1)} %get-tuple-element.25), channel_id=1, source_target_pairs={{0,2},{1,3},{2,0},{3,1},{8,10},{9,11},{10,8},{11,9},{4,6},{5,7},{6... | collective-permute-start | bytes 313352 | tf_op jit(solution)/shard_map/ppermute | solution.py:462
  17.6 12.7 %collective-permute-start.3 = (bf16[24,2176]{1,0:T(8,128)(2,1)}, bf16[24,2176]{1,0:T(8,128)(2,1)S(1)}, u32[]{:S(2)}, u32[]{:S(2)}) collective-permute-start(bf16[24,2176]{1,0:T(8,128)(2,1)} %get-tuple-element.26), channel_id=1, source_target_pairs={{0,8},{1,9},{2,10},{3,11},{8,0},{9,1},{10,2},{11,3},{4,12},{5,13},... | collective-permute-start | bytes 313352 | tf_op jit(solution)/shard_map/ppermute | solution.py:462
  23.6 3.1 %collective-permute-start.7 = (bf16[16,4,2176]{2,0,1:T(8,128)(2,1)S(1)}, bf16[16,4,2176]{2,0,1:T(8,128)(2,1)S(1)}, u32[]{:S(2)}, u32[]{:S(2)}) collective-permute-start(bf16[16,4,2176]{2,0,1:T(8,128)(2,1)S(1)} %copy.25), channel_id=1, source_target_pairs={{0,4},{4,0},{1,5},{5,1},{2,6},{6,2},{3,7},{7,3},{8,12},{12,8},{9,1... | collective-permute-start | bytes 835592 | tf_op jit(solution)/shard_map/ppermute | solution.py:458
  24.5 7.7 %collective-permute-start.4 = (bf16[24,2176]{1,0:T(8,128)(2,1)}, bf16[24,2176]{1,0:T(8,128)(2,1)S(1)}, u32[]{:S(2)}, u32[]{:S(2)}) collective-permute-start(bf16[24,2176]{1,0:T(8,128)(2,1)} %get-tuple-element.27), channel_id=1, source_target_pairs={{0,3},{1,2},{2,1},{3,0},{8,11},{9,10},{10,9},{11,8},{4,7},{5,6},{6... | collective-permute-start | bytes 313352 | tf_op jit(solution)/shard_map/ppermute | solution.py:462
  24.8 7.5 %collective-permute-start.5 = (bf16[24,2176]{1,0:T(8,128)(2,1)}, bf16[24,2176]{1,0:T(8,128)(2,1)S(1)}, u32[]{:S(2)}, u32[]{:S(2)}) collective-permute-start(bf16[24,2176]{1,0:T(8,128)(2,1)} %get-tuple-element.28), channel_id=1, source_target_pairs={{0,9},{1,8},{2,11},{3,10},{8,1},{9,0},{10,3},{11,2},{4,13},{5,12},... | collective-permute-start | bytes 313352 | tf_op jit(solution)/shard_map/ppermute | solution.py:462
  26.7 7.4 %collective-permute-start.6 = (bf16[24,2176]{1,0:T(8,128)(2,1)}, bf16[24,2176]{1,0:T(8,128)(2,1)S(1)}, u32[]{:S(2)}, u32[]{:S(2)}) collective-permute-start(bf16[24,2176]{1,0:T(8,128)(2,1)} %get-tuple-element.29), channel_id=1, source_target_pairs={{0,10},{1,11},{2,8},{3,9},{8,2},{9,3},{10,0},{11,1},{4,14},{5,15},... | collective-permute-start | bytes 313352 | tf_op jit(solution)/shard_map/ppermute | solution.py:462
  48.5 1.6 %collective-permute-start.8 = (bf16[4,16,2176]{2,0,1:T(4,128)(2,1)S(1)}, bf16[4,16,2176]{2,0,1:T(4,128)(2,1)S(1)}, u32[]{:S(2)}, u32[]{:S(2)}) collective-permute-start(bf16[4,16,2176]{2,0,1:T(4,128)(2,1)S(1)} %copy.16), channel_id=1, source_target_pairs={{0,4},{4,0},{1,5},{5,1},{2,6},{6,2},{3,7},{7,3},{8,12},{12,8},{9,1... | collective-permute-start | bytes 835592 | tf_op jit(solution)/shard_map/ppermute | solution.py:518
  51.1 14.4 %all-to-all-start.2 = ((bf16[16,4,2176]{2,1,0:T(4,128)(2,1)}), bf16[16,4,2176]{2,1,0:T(4,128)(2,1)S(1)}, u32[]{:S(2)}, u32[]{:S(2)}) async-start(bf16[16,4,2176]{2,1,0:T(4,128)(2,1)} %fusion.1), calls=%async_computation.2 | async-start | bytes 557056 | tf_op jit(solution)/shard_map/all_to_all | solution.py:535

commit v5 on v4

--- a/solution.py
+++ b/solution.py
@@ -307,12 +307,13 @@
     width = phases.shape[1]
     held, peers = out.shape[0] // 2, out.shape[1]
     total = held * peers
-    chunk = 2 * LANES
+    weights = jnp.concatenate([weights_real, weights_imag], axis=0)
+    chunk = 6 * LANES
     for low in range(0, width, chunk):
         high = min(low + chunk, width)
         images = aligned[:, low:high]
-        real = jnp.dot(weights_real, images, preferred_element_type=f32)
-        imag = jnp.dot(weights_imag, images, preferred_element_type=f32)
+        both = jnp.dot(weights, images, preferred_element_type=f32)
+        real, imag = both[: SHIFTS * total], both[SHIFTS * total :]
         u = [real[t * total : (t + 1) * total] for t in range(SHIFTS)]
         v = [imag[t * total : (t + 1) * total] for t in range(SHIFTS)]
         first, second = u[0], v[0]

time: 66.7 us -> 66.7 us (level)
  no operation moved by 1% of the time
where the time goes in v5:
time: 66.7 us; the launch traced here: 66.4 us
  starting transfers between devices  21.6 us (32%)
  waiting for transfers between devices  21.2 us (32%)
  blocking collectives  11.2 us (17%)
  Pallas kernels  9.23 us (14%)
  other arithmetic  1.6 us (2%)
  local copies, waits for them, and re-layouts  0.81 us (1%)
  between operations  0.77 us (1%)
    all_to_all x1, blocking collectives, expectation(): lax.all_to_all(scores, group, split_axis=0, concat_axis=0, tiled=True)  11.2 us
    all_to_all x1, waiting for transfers between devices, expectation(): lax.all_to_all(merged, same_core, split_axis=0, concat_axis=0, tiled=True)  10.3 us
    ppermute x7, starting transfers between devices, expectation(): parts[at] = lax.ppermute(parts[at], group, routes_of(steps[at], pieces))  9.4 us
    all_to_all x1, starting transfers between devices, expectation(): lax.all_to_all(refs, same_core, split_axis=0, concat_axis=0, tiled=True)  8.49 us
    all_to_all x1, waiting for transfers between devices, expectation(): lax.all_to_all(refs, same_core, split_axis=0, concat_axis=0, tiled=True)  5.75 us
    ppermute x7, waiting for transfers between devices, expectation(): parts[at] = lax.ppermute(parts[at], group, routes_of(steps[at], pieces))  4.26 us
    pallas_call x1, Pallas kernels, expectation(): pl.pallas_call(functools.partial(prepare_kernel, pixel_count, plan, steps...  3.56 us
    all_to_all x1, starting transfers between devices, expectation(): lax.all_to_all(merged, same_core, split_axis=0, concat_axis=0, tiled=True)  3.53 us
  transfers between devices with their start and end apart: 11, of which 6 were waited for; matrix products, arithmetic and copies ran while one was open for 2% of the time, Pallas kernels for 3%

profile of v5, /device:TPU:0, one launch (start us, length us, event | category | flops | bytes accessed | tf_op | source)
XLA Modules:
  0.0 66.4 jit_solution(4453932970936867877)
XLA Ops:
  0.6 3.6 %prepare.1 = (bf16[16,4,2176]{2,1,0:T(4,128)(2,1)}, bf16[8,2176]{1,0:T(8,128)(2,1)}, bf16[24,2176]{1,0:T(8,128)(2,1)}, bf16[24,2176]{1,0:T(8,128)(2,1)}, bf16[24...) custom-call(bf16[2,33024]{1,0:T(2,128)(2,1)} %bitcast.19, ...), custom_call_target="tpu_custom_call" | custom-call | tf_op jit(solution)/shard_map/prepare/pallas_call | solution.py:440
  4.2 0.0 copy-start.1
  4.2 8.5 %all-to-all-start = ((bf16[16,4,2176]{2,1,0:T(4,128)(2,1)}), bf16[16,4,2176]{2,1,0:T(4,128)(2,1)S(1)}, u32[]{:S(2)}, u32[]{:S(2)}) async-start(bf16[16,4,2176]{2,1,0:T(4,128)(2,1)} %get-tuple-element.30), calls=%async_computation | async-start | bytes 557056 | tf_op jit(solution)/shard_map/all_to_all | solution.py:458
  12.7 3.7 %collective-permute-start = (bf16[24,2176]{1,0:T(8,128)(2,1)}, bf16[24,2176]{1,0:T(8,128)(2,1)S(1)}, u32[]{:S(2)}, u32[]{:S(2)}) collective-permute-start(bf16[24,2176]{1,0:T(8,128)(2,1)} %get-tuple-element.23), channel_id=1, source_target_pairs={{0,11},{1,10},{2,9},{3,8},{8,3},{9,2},{10,1},{11,0},{4,15},{5,14},... | collective-permute-start | bytes 313352 | tf_op jit(solution)/shard_map/ppermute | solution.py:463
  16.4 0.6 collective-permute-start.1
  17.0 0.6 collective-permute-start.2
  17.6 0.2 collective-permute-start.3
  17.7 0.1 fusion.5
  17.8 5.8 %all-to-all-done = bf16[16,4,2176]{2,1,0:T(4,128)(2,1)S(1)} async-done(((bf16[16,4,2176]{2,1,0:T(4,128)(2,1)}), bf16[16,4,2176]{2,1,0:T(4,128)(2,1)S(1)}, u32[]{:S(2)}, u32[]{:S(2)}) %all-to-all-start) | async-done | bytes 278560 | tf_op jit(solution)/shard_map/all_to_all | solution.py:458
  23.6 0.1 collective-permute-start.7
  23.7 0.5 fusion.8
  24.2 0.3 collective-permute-done.refs_all_1_
  24.5 0.2 collective-permute-start.4
  24.8 0.0 collective-permute-done.1.refs_all_2_
  24.8 2.0 %collective-permute-start.5 = (bf16[24,2176]{1,0:T(8,128)(2,1)}, bf16[24,2176]{1,0:T(8,128)(2,1)S(1)}, u32[]{:S(2)}, u32[]{:S(2)}) collective-permute-start(bf16[24,2176]{1,0:T(8,128)(2,1)} %get-tuple-element.28), channel_id=1, source_target_pairs={{0,9},{1,8},{2,11},{3,10},{8,1},{9,0},{10,3},{11,2},{4,13},{5,12},... | collective-permute-start | bytes 313352 | tf_op jit(solution)/shard_map/ppermute | solution.py:463
  26.7 2.2 %collective-permute-start.6 = (bf16[24,2176]{1,0:T(8,128)(2,1)}, bf16[24,2176]{1,0:T(8,128)(2,1)S(1)}, u32[]{:S(2)}, u32[]{:S(2)}) collective-permute-start(bf16[24,2176]{1,0:T(8,128)(2,1)} %get-tuple-element.29), channel_id=1, source_target_pairs={{0,10},{1,11},{2,8},{3,9},{8,2},{9,3},{10,0},{11,1},{4,14},{5,15},... | collective-permute-start | bytes 313352 | tf_op jit(solution)/shard_map/ppermute | solution.py:463
  29.0 0.6 shard_map.77
  29.6 0.6 shard_map.78
  30.3 2.0 %collective-permute-done.4.refs_all_5_ = bf16[24,2176]{1,0:T(8,128)(2,1)S(1)} collective-permute-done((bf16[24,2176]{1,0:T(8,128)(2,1)}, bf16[24,2176]{1,0:T(8,128)(2,1)S(1)}, u32[]{:S(2)}, u32[]{:S(2)}) %collective-permute-start.4) | collective-permute-done | bytes 104480 | tf_op jit(solution)/shard_map/ppermute | solution.py:463
  32.3 1.9 %collective-permute-done.6.refs_all_7_ = bf16[24,2176]{1,0:T(8,128)(2,1)S(1)} collective-permute-done((bf16[24,2176]{1,0:T(8,128)(2,1)}, bf16[24,2176]{1,0:T(8,128)(2,1)S(1)}, u32[]{:S(2)}, u32[]{:S(2)}) %collective-permute-start.6) | collective-permute-done | bytes 104480 | tf_op jit(solution)/shard_map/ppermute | solution.py:463
  34.2 1.8 %score.1 = (f32[8,24,640]{2,1,0:T(8,128)S(1)}, bf16[8,24,2176]{2,1,0:T(8,128)(2,1)S(1)}) custom-call(bf16[24,2176]{1,0:T(8,128)(2,1)S(1)} %copy-done.1, bf16[24,2176]{1,0:T(8,128)(2,1)S(1)} %collective-permute-done.refs_all_1_, bf16[24,2176]{1,0:T(8,128)(2,1)S(1)} %collective-permute-done.1.refs_all_2_, ...), custom_call_target="tpu_custom_call" | custom-call | tf_op jit(solution)/shard_map/score/pallas_call | solution.py:487
  36.0 11.2 %all_to_all.15.scores = f32[8,24,640]{2,1,0:T(8,128)S(1)} all-to-all(f32[8,24,640]{2,1,0:T(8,128)S(1)} %get-tuple-element.36), channel_id=1, replica_groups=mesh['groups'=1,'far'=2,'near'=2,'core'=2,'cls'=4] {'near','cls'}, dimensions={0} | all-to-all | bytes 983040 | tf_op jit(solution)/shard_map/all_to_all | solution.py:503
  47.1 1.3 %weigh.1 = (bf16[4,16,2176]{2,1,0:T(8,128)(2,1)S(1)}, bf16[160,192]{1,0:T(8,128)(2,1)S(1)}, bf16[160,192]{1,0:T(8,128)(2,1)S(1)}, f32[192,128]{1,0:T(8,128)S(1)}) custom-call(f32[8,24,640]{2,1,0:T(8,128)S(1)} %all_to_all.15.scores, bf16[192,2176]{1,0:T(8,128)(2,1)S(1)} %bitcast.15, f32[4,2176]{1,0:T(4,128)S(1)} %reshape.113.phases), custom_call_target="tpu_custom_call" | custom-call | tf_op jit(solution)/shard_map/weigh/pallas_call | solution.py:507
  48.5 0.1 copy.16
  48.6 0.1 collective-permute-start.8
  48.7 0.6 own.1
  49.3 0.9 %collective-permute-done.8 = bf16[4,16,2176]{2,0,1:T(4,128)(2,1)S(1)} collective-permute-done((bf16[4,16,2176]{2,0,1:T(4,128)(2,1)S(1)}, bf16[4,16,2176]{2,0,1:T(4,128)(2,1)S(1)}, u32[]{:S(2)}, u32[]{:S(2)}) %collective-permute-start.8) | collective-permute-done | bytes 278560 | tf_op jit(solution)/shard_map/ppermute | solution.py:519
  50.2 1.0 %fusion.1 = bf16[16,4,2176]{2,1,0:T(4,128)(2,1)} fusion(bf16[4,16,2176]{2,0,1:T(4,128)(2,1)S(1)} %collective-permute-done.8, f32[4,16,2176]{2,1,0:T(8,128)S(1)} %own.1), kind=kLoop, calls=%fused_computation.2 | loop fusion | flops 417792 | bytes 1114112 | tf_op jit(solution)/shard_map/transpose | solution.py:535
  51.2 3.5 %all-to-all-start.2 = ((bf16[16,4,2176]{2,1,0:T(4,128)(2,1)}), bf16[16,4,2176]{2,1,0:T(4,128)(2,1)S(1)}, u32[]{:S(2)}, u32[]{:S(2)}) async-start(bf16[16,4,2176]{2,1,0:T(4,128)(2,1)} %fusion.1), calls=%async_computation.2 | async-start | bytes 557056 | tf_op jit(solution)/shard_map/all_to_all | solution.py:536
  54.7 0.6 dynamic-slice_reduce_fusion
  55.4 10.3 %all-to-all-done.2.parts = bf16[16,4,2176]{2,1,0:T(4,128)(2,1)S(1)} async-done(((bf16[16,4,2176]{2,1,0:T(4,128)(2,1)}), bf16[16,4,2176]{2,1,0:T(4,128)(2,1)S(1)}, u32[]{:S(2)}, u32[]{:S(2)}) %all-to-all-start.2) | async-done | bytes 278560 | tf_op jit(solution)/shard_map/all_to_all | solution.py:536
  65.6 0.7 %collect.1 = bf16[2,33024]{1,0:T(2,128)(2,1)} custom-call(bf16[16,4,2176]{2,1,0:T(4,128)(2,1)S(1)} %all-to-all-done.2.parts), custom_call_target="tpu_custom_call" | custom-call | tf_op jit(solution)/shard_map/collect/pallas_call | solution.py:537
  (10 shorter events, 0.1 us)
Async XLA Ops:
  4.2 24.8 %copy-start = (bf16[8,2176]{1,0:T(8,128)(2,1)S(1)}, bf16[8,2176]{1,0:T(8,128)(2,1)}, u32[]{:S(2)}) copy-start(bf16[8,2176]{1,0:T(8,128)(2,1)} %get-tuple-element.31.ctf) | copy-start | bytes 104452
  4.2 30.0 %copy-start.1 = (bf16[24,2176]{1,0:T(8,128)(2,1)S(1)}, bf16[24,2176]{1,0:T(8,128)(2,1)}, u32[]{:S(2)}) copy-start(bf16[24,2176]{1,0:T(8,128)(2,1)} %get-tuple-element.22.refs_all_0_) | copy-start | bytes 313348
  4.2 19.3 %all-to-all-start = ((bf16[16,4,2176]{2,1,0:T(4,128)(2,1)}), bf16[16,4,2176]{2,1,0:T(4,128)(2,1)S(1)}, u32[]{:S(2)}, u32[]{:S(2)}) async-start(bf16[16,4,2176]{2,1,0:T(4,128)(2,1)} %get-tuple-element.30), calls=%async_computation | async-start | bytes 557056 | tf_op jit(solution)/shard_map/all_to_all | solution.py:458
  12.7 11.8 %collective-permute-start = (bf16[24,2176]{1,0:T(8,128)(2,1)}, bf16[24,2176]{1,0:T(8,128)(2,1)S(1)}, u32[]{:S(2)}, u32[]{:S(2)}) collective-permute-start(bf16[24,2176]{1,0:T(8,128)(2,1)} %get-tuple-element.23), channel_id=1, source_target_pairs={{0,11},{1,10},{2,9},{3,8},{8,3},{9,2},{10,1},{11,0},{4,15},{5,14},... | collective-permute-start | bytes 313352 | tf_op jit(solution)/shard_map/ppermute | solution.py:463
  16.4 8.3 %collective-permute-start.1 = (bf16[24,2176]{1,0:T(8,128)(2,1)}, bf16[24,2176]{1,0:T(8,128)(2,1)S(1)}, u32[]{:S(2)}, u32[]{:S(2)}) collective-permute-start(bf16[24,2176]{1,0:T(8,128)(2,1)} %get-tuple-element.24), channel_id=1, source_target_pairs={{0,1},{1,0},{2,3},{3,2},{8,9},{9,8},{10,11},{11,10},{4,5},{5,4},{6... | collective-permute-start | bytes 313352 | tf_op jit(solution)/shard_map/ppermute | solution.py:463
  17.0 13.2 %collective-permute-start.2 = (bf16[24,2176]{1,0:T(8,128)(2,1)}, bf16[24,2176]{1,0:T(8,128)(2,1)S(1)}, u32[]{:S(2)}, u32[]{:S(2)}) collective-permute-start(bf16[24,2176]{1,0:T(8,128)(2,1)} %get-tuple-element.25), channel_id=1, source_target_pairs={{0,2},{1,3},{2,0},{3,1},{8,10},{9,11},{10,8},{11,9},{4,6},{5,7},{6... | collective-permute-start | bytes 313352 | tf_op jit(solution)/shard_map/ppermute | solution.py:463
  17.6 12.7 %collective-permute-start.3 = (bf16[24,2176]{1,0:T(8,128)(2,1)}, bf16[24,2176]{1,0:T(8,128)(2,1)S(1)}, u32[]{:S(2)}, u32[]{:S(2)}) collective-permute-start(bf16[24,2176]{1,0:T(8,128)(2,1)} %get-tuple-element.26), channel_id=1, source_target_pairs={{0,8},{1,9},{2,10},{3,11},{8,0},{9,1},{10,2},{11,3},{4,12},{5,13},... | collective-permute-start | bytes 313352 | tf_op jit(solution)/shard_map/ppermute | solution.py:463
  23.6 3.1 %collective-permute-start.7 = (bf16[16,4,2176]{2,0,1:T(8,128)(2,1)S(1)}, bf16[16,4,2176]{2,0,1:T(8,128)(2,1)S(1)}, u32[]{:S(2)}, u32[]{:S(2)}) collective-permute-start(bf16[16,4,2176]{2,0,1:T(8,128)(2,1)S(1)} %copy.25), channel_id=1, source_target_pairs={{0,4},{4,0},{1,5},{5,1},{2,6},{6,2},{3,7},{7,3},{8,12},{12,8},{9,1... | collective-permute-start | bytes 835592 | tf_op jit(solution)/shard_map/ppermute | solution.py:459
  24.5 7.7 %collective-permute-start.4 = (bf16[24,2176]{1,0:T(8,128)(2,1)}, bf16[24,2176]{1,0:T(8,128)(2,1)S(1)}, u32[]{:S(2)}, u32[]{:S(2)}) collective-permute-start(bf16[24,2176]{1,0:T(8,128)(2,1)} %get-tuple-element.27), channel_id=1, source_target_pairs={{0,3},{1,2},{2,1},{3,0},{8,11},{9,10},{10,9},{11,8},{4,7},{5,6},{6... | collective-permute-start | bytes 313352 | tf_op jit(solution)/shard_map/ppermute | solution.py:463
  24.8 7.5 %collective-permute-start.5 = (bf16[24,2176]{1,0:T(8,128)(2,1)}, bf16[24,2176]{1,0:T(8,128)(2,1)S(1)}, u32[]{:S(2)}, u32[]{:S(2)}) collective-permute-start(bf16[24,2176]{1,0:T(8,128)(2,1)} %get-tuple-element.28), channel_id=1, source_target_pairs={{0,9},{1,8},{2,11},{3,10},{8,1},{9,0},{10,3},{11,2},{4,13},{5,12},... | collective-permute-start | bytes 313352 | tf_op jit(solution)/shard_map/ppermute | solution.py:463
  26.7 7.4 %collective-permute-start.6 = (bf16[24,2176]{1,0:T(8,128)(2,1)}, bf16[24,2176]{1,0:T(8,128)(2,1)S(1)}, u32[]{:S(2)}, u32[]{:S(2)}) collective-permute-start(bf16[24,2176]{1,0:T(8,128)(2,1)} %get-tuple-element.29), channel_id=1, source_target_pairs={{0,10},{1,11},{2,8},{3,9},{8,2},{9,3},{10,0},{11,1},{4,14},{5,15},... | collective-permute-start | bytes 313352 | tf_op jit(solution)/shard_map/ppermute | solution.py:463
  48.6 1.6 %collective-permute-start.8 = (bf16[4,16,2176]{2,0,1:T(4,128)(2,1)S(1)}, bf16[4,16,2176]{2,0,1:T(4,128)(2,1)S(1)}, u32[]{:S(2)}, u32[]{:S(2)}) collective-permute-start(bf16[4,16,2176]{2,0,1:T(4,128)(2,1)S(1)} %copy.16), channel_id=1, source_target_pairs={{0,4},{4,0},{1,5},{5,1},{2,6},{6,2},{3,7},{7,3},{8,12},{12,8},{9,1... | collective-permute-start | bytes 835592 | tf_op jit(solution)/shard_map/ppermute | solution.py:519
  51.2 14.4 %all-to-all-start.2 = ((bf16[16,4,2176]{2,1,0:T(4,128)(2,1)}), bf16[16,4,2176]{2,1,0:T(4,128)(2,1)S(1)}, u32[]{:S(2)}, u32[]{:S(2)}) async-start(bf16[16,4,2176]{2,1,0:T(4,128)(2,1)} %fusion.1), calls=%async_computation.2 | async-start | bytes 557056 | tf_op jit(solution)/shard_map/all_to_all | solution.py:536
